TPU v7x, 256 devices: a whole 4x4x8 slice. The times are simulated.
256 devices in a mesh: grp: 16 (over z, x_hi), wide: 16 (over y, x_lo, core).
Axes of the slice: x: 4 (x_hi: 2, x_lo: 2; x = x_hi * 2 + x_lo), y: 4, z: 8, core: 2. Of those that a mesh axis runs over, the one named last changes fastest.
Arguments:
- velocity: float32 [3, 1024, 128, 128], P(None, 'grp', 'wide'), may hold values from -6 to 6
- coarse_ghost: float32 [3, 1024, 32, 128], P(None, 'grp', 'wide'), may hold values from -6 to 6
- viscosity: float32 [1024, 128, 128], P('grp', 'wide'), may hold values from 0.5 to 4
- stress: float32 [6, 1024, 128, 128], P(None, 'grp', 'wide'), may hold values from -6 to 6
- patch_mask: int32 [16, 32], P('grp', 'wide'), may hold values 0 or 1
- coarse_owner: int32 [16, 32], P('grp', 'wide'), may hold values from 0 to 255, as said below
Outputs:
- new_velocity: float32 [3, 1024, 128, 128], P(None, 'grp', 'wide')
- coarse_patch_update: float32 [16, 256, 3, 6144], P('grp', 'wide')
Inputs may be any that keep to these rules, and one draw needn't show every extreme that they name: `coarse_owner`: coarse patch c belongs to wide index c // 16. Of the 2 fine patches of one device at most 1 have coarse patches on any one wide index, and in every draw every device sends exactly 1 to one common wide index.
All inputs are finite; a program needn't handle non-finite values. No bound on the sum of `patch_mask` on one device may be relied on, other than what follows from the above.
Results may differ from a plain program's by a relative error of at most 0.000096.
Values sent between devices are 32-bit elements; how exact they have to be, the bound alone decides.
A program may use at most 128 MiB of HBM per device.

v0:
```python
import jax
import jax.numpy as jnp
from jax import lax
from jax.sharding import PartitionSpec as P

PATCH = 64
CY = 8
P_SIZE = 2
CP_DEV = 16
SWEEPS = 3
CAP = 1
PV = 6144


KAPPA = 1.0
OMEGA = 0.8


def with_halo(block, sides, width):
    for axis, dim in sides:
        count = lax.axis_size(axis)
        forward = [(i, i + 1) for i in range(count - 1)]
        backward = [(target, source) for source, target in forward]
        low = lax.ppermute(
            lax.slice_in_dim(block, block.shape[dim] - width, None, axis=dim), axis, forward
        )
        high = lax.ppermute(lax.slice_in_dim(block, 0, width, axis=dim), axis, backward)
        block = jnp.concatenate([low, block, high], axis=dim)
    return block


def y_neighbours(field, low, high):
    ypos = lax.broadcasted_iota(jnp.int32, field.shape, field.ndim - 2)
    last_row = field.shape[-2] - 1
    north = jnp.where(ypos == last_row, jnp.expand_dims(high, -2), jnp.roll(field, -1, axis=-2))
    south = jnp.where(ypos == 0, jnp.expand_dims(low, -2), jnp.roll(field, 1, axis=-2))
    return (north, south)


def apply_operator(values_x, ghost_rows, visc_x):
    centre_cell = visc_x[1:-1]
    visc_east = 0.5 * (centre_cell + visc_x[2:])
    visc_west = 0.5 * (centre_cell + visc_x[:-2])
    visc_n, visc_s = y_neighbours(centre_cell, centre_cell[:, 0, :], centre_cell[:, -1, :])
    visc_north = 0.5 * (centre_cell + visc_n)
    visc_south = 0.5 * (centre_cell + visc_s)
    visc_up = 0.5 * (centre_cell + jnp.roll(centre_cell, -1, axis=2))
    visc_down = 0.5 * (centre_cell + jnp.roll(centre_cell, 1, axis=2))
    interior = values_x[:, 1:-1]
    north_vals, south_vals = y_neighbours(interior, ghost_rows[:, :, 0, :], ghost_rows[:, :, 1, :])
    diffusion = visc_east * (values_x[:, 2:] - interior) - visc_west * (interior - values_x[:, :-2])
    diffusion = (
        diffusion + visc_north * (north_vals - interior) - visc_south * (interior - south_vals)
    )
    diffusion = (
        diffusion
        + visc_up * (jnp.roll(interior, -1, axis=3) - interior)
        - visc_down * (interior - jnp.roll(interior, 1, axis=3))
    )
    diagonal = KAPPA + visc_east + visc_west + visc_north + visc_south + visc_up + visc_down
    return (KAPPA * interior - diffusion, diagonal)


def divergence(stress_x):

    def diff_x(comp):
        return 0.5 * (comp[2:] - comp[:-2])

    def diff_y(comp):
        middle = comp[1:-1]
        zeros_row = jnp.zeros_like(middle[:, 0, :])
        north_vals, south_vals = y_neighbours(middle, zeros_row, zeros_row)
        return 0.5 * (north_vals - south_vals)

    def diff_z(comp):
        middle = comp[1:-1]
        return 0.5 * (jnp.roll(middle, -1, axis=2) - jnp.roll(middle, 1, axis=2))

    force_x = diff_x(stress_x[0]) + diff_y(stress_x[3]) + diff_z(stress_x[4])
    force_y = diff_x(stress_x[3]) + diff_y(stress_x[1]) + diff_z(stress_x[5])
    force_z = diff_x(stress_x[4]) + diff_y(stress_x[5]) + diff_z(stress_x[2])
    return jnp.stack([force_x, force_y, force_z], axis=0)


def patch_data(residual, smoothed, viscosity, coarse_ghost, groups):
    half = PATCH // 2
    blocks = residual.reshape(3, groups, half, 2, CY // 2, 2, P_SIZE, half, 2).mean(axis=(3, 5, 8))
    blocks = jnp.transpose(blocks, (1, 4, 0, 2, 3, 5)).reshape(
        groups, P_SIZE, 3, half * (CY // 2) * half
    )
    flux_low = viscosity[:, 0, :] * (smoothed[:, :, 0, :] - coarse_ghost[:, :, 0, :])
    flux_high = viscosity[:, -1, :] * (coarse_ghost[:, :, 1, :] - smoothed[:, :, -1, :])

    def faces(flux):
        reduced_terms = flux.reshape(3, groups, half, 2, P_SIZE, half, 2).mean(axis=(3, 6))
        return jnp.transpose(reduced_terms, (1, 3, 0, 2, 4)).reshape(groups, P_SIZE, 3, half * half)

    return jnp.concatenate([blocks, faces(flux_low), faces(flux_high)], axis=3)


def on_device(velocity, coarse_ghost, viscosity, stress, patch_mask, coarse_owner):
    cells_x = velocity.shape[1]
    margin = SWEEPS + 1
    stacked = with_halo(
        jnp.concatenate([velocity, stress, viscosity[None]], axis=0), (("grp", 1),), margin
    )
    ghost_ext = with_halo(coarse_ghost, (("grp", 1),), margin)
    vel_ext = stacked[:3]
    visc_ext = stacked[9]
    span = visc_ext.shape[0]
    source = KAPPA * vel_ext[:, 1:-1] + divergence(stacked[3:9])
    rows = source.shape[1]
    total_x = cells_x * lax.axis_size("grp")
    first_cell = lax.axis_index("grp") * cells_x
    for sweep_index in range(SWEEPS):
        ghost_rows = ghost_ext[:, sweep_index + 1 : span - sweep_index - 1]
        applied, diagonal = apply_operator(
            vel_ext, ghost_rows, visc_ext[sweep_index : span - sweep_index]
        )
        source_part = source[:, sweep_index : rows - sweep_index]
        patch_positions = (
            first_cell - (margin - 1 - sweep_index) + jnp.arange(applied.shape[1], dtype=jnp.int32)
        )
        inside = ((patch_positions >= 0) & (patch_positions < total_x)).astype(jnp.float32)
        interior = vel_ext[:, 1:-1]
        vel_ext = (
            interior + OMEGA * (source_part - applied) / diagonal * inside[None, :, None, None]
        )
    ghost_rows = ghost_ext[:, SWEEPS + 1 : span - SWEEPS - 1]
    applied, diagonal = apply_operator(vel_ext, ghost_rows, visc_ext[SWEEPS : span - SWEEPS])
    residual = source[:, SWEEPS : rows - SWEEPS] - applied
    smoothed = vel_ext[:, 1:-1]
    fine_patches = patch_data(residual, smoothed, viscosity, coarse_ghost, 1).reshape(
        P_SIZE, 3 * PV
    )
    fine_patches = fine_patches * patch_mask[0][:, None].astype(jnp.float32)
    owner_row = coarse_owner[0]
    wide_count = lax.axis_size("wide")
    slot_count = wide_count * CAP
    target = owner_row // CP_DEV
    local_index = owner_row % CP_DEV
    patch_order = jnp.arange(P_SIZE, dtype=jnp.int32)
    earlier = jnp.sum(
        (
            (target[None, :] == target[:, None]) & (patch_order[None, :] < patch_order[:, None])
        ).astype(jnp.int32),
        axis=1,
    )
    slot_index = target * CAP + earlier
    slot_lattice = jnp.arange(slot_count, dtype=jnp.int32)
    placement = slot_index[None, :] == slot_lattice[:, None]
    buffer = jnp.dot(
        placement.astype(jnp.float32), fine_patches, precision=lax.Precision.HIGHEST
    ).reshape(wide_count, CAP, 3 * PV)
    labels = (jnp.sum(jnp.where(placement, local_index[None, :] + 1, 0), axis=1) - 1).reshape(
        wide_count, CAP
    )
    received_terms, coarse_ids = (
        lax.all_to_all(buffer, "wide", split_axis=0, concat_axis=0, tiled=True),
        lax.all_to_all(labels, "wide", split_axis=0, concat_axis=0, tiled=True),
    )
    indicator_matrix = (
        coarse_ids.reshape(-1)[None, :] == jnp.arange(CP_DEV, dtype=jnp.int32)[:, None]
    ).astype(jnp.float32)
    coarse = jnp.dot(
        indicator_matrix,
        received_terms.reshape(slot_count, 3 * PV),
        precision=lax.Precision.HIGHEST,
    )
    return (smoothed, coarse.reshape(1, CP_DEV, 3, PV))


def solution(mesh):
    in_specs = (
        P(None, "grp", "wide", None),
        P(None, "grp", "wide", None),
        P("grp", "wide", None),
        P(None, "grp", "wide", None),
        P("grp", "wide"),
        P("grp", "wide"),
    )
    out_specs = (P(None, "grp", "wide", None), P("grp", "wide", None, None))
    return jax.shard_map(
        on_device, mesh=mesh, in_specs=in_specs, out_specs=out_specs, check_vma=False
    )
```

profile of v0, /device:TPU:1, one launch (start us, length us, event | category | flops | bytes accessed | tf_op | source)
XLA Modules:
  0.0 201.3 jit_solution(4859155737020148961)
XLA Ops:
  0.6 1.1 copy.229
  1.7 1.7 copy.190
  3.6 0.8 pad_maximum_fusion.10
  4.4 1.3 collective-permute-start.1
  5.7 6.1 %collective-permute-start = (f32[10,4,8,128]{3,1,2,0:T(4,128)}, f32[10,4,8,128]{3,1,2,0:T(4,128)S(1)}, u32[]{:S(2)}, u32[]{:S(2)}) collective-permute-start(f32[10,4,8,128]{3,1,2,0:T(4,128)} %get-tuple-element.55), channel_id=1, source_target_pairs={{0,16},{16,32},{32,48},{48,64},{64,80},{80,96},{96,112},{112,128},... | collective-permute-start | bytes 491528 | tf_op jit(solution)/shard_map/ppermute | solution.py:24
  11.9 0.7 fusion.164
  12.6 1.3 collective-permute-start.3
  13.9 7.0 %collective-permute-start.2 = (f32[3,4,2,128]{3,1,0,2:T(4,128)}, f32[3,4,2,128]{3,1,0,2:T(4,128)}, u32[]{:S(2)}, u32[]{:S(2)}) collective-permute-start(f32[3,4,2,128]{3,1,0,2:T(4,128)} %get-tuple-element.157), channel_id=1, source_target_pairs={{0,16},{16,32},{32,48},{48,64},{64,80},{80,96},{96,112},{112,128},... | collective-permute-start | bytes 36872 | tf_op jit(solution)/shard_map/ppermute | solution.py:24
  21.8 0.7 copy.206
  22.4 6.6 %all-to-all-start = ((s32[16,1,1]{2,1,0:T(1,128)}), s32[16,1,1]{2,1,0:T(1,128)}, u32[]{:S(2)}, u32[]{:S(2)}) async-start(s32[16,1,1]{2,1,0:T(1,128)} %copy.206), calls=%async_computation | async-start | bytes 16384 | tf_op jit(solution)/shard_map/all_to_all | solution.py:160
  29.0 1.9 fusion.163
  30.9 0.8 slice_reduce_fusion
  31.7 0.8 fusion.160
  32.5 0.9 fusion.162
  33.4 0.9 fusion.161
  34.3 2.5 %fusion.111 = (f32[64,8,128]{2,1,0:T(8,128)S(1)}, f32[64,8,128]{2,1,0:T(8,128)}, f32[64,8,128]{2,1,0:T(8,128)}, f32[64,8,128]{2,1,0:T(8,128)}) fusion(f32[64,8,128]{2,1,0:T(8,128)S(1)} %copy-done, f32[64,1,128]{2,1,0:T(1,128)S(1)} %get-tuple-element.143, f32[64,7,128]{2,1,0:T(8,128)} %get-tuple-element.141, f32[64,128]{1,0:T(8,128)S(1)} %bitcast.274, ...), kind=kLoop, calls=%fused_computation.214 | loop fusion | flops 917504 | bytes 2424848 | tf_op jit(solution)/shard_map/mul | solution.py:45
  36.8 4.2 %mul.571 = f32[32,2,2,32,2]{4,3,2,1,0:T(8,128)} reshape(f32[64,128]{1,0:T(8,128)} %get-tuple-element.13) | data formatting | bytes 65536 | tf_op jit(solution)/shard_map/mul | solution.py:92
  41.0 4.2 %mul.568 = f32[32,2,2,32,2]{4,3,2,1,0:T(8,128)} reshape(f32[64,128]{1,0:T(8,128)} %get-tuple-element.12) | data formatting | bytes 65536 | tf_op jit(solution)/shard_map/mul | solution.py:91
  45.2 1.7 copy.212
  46.9 1.7 copy.211
  48.6 0.8 copy.209
  49.4 0.7 copy.207
  50.1 1.0 pad_maximum_fusion.7
  55.4 1.7 multiply_add_fusion.2
  58.9 1.3 multiply_add_fusion.1
  62.1 1.3 multiply_add_fusion
  63.4 1.3 fusion.151
  64.7 1.4 fusion.148
  66.1 1.5 fusion.149
  67.6 0.8 fusion.150
  68.4 8.4 %sub.321 = f32[3,1,32,2,2,32,2]{6,5,4,3,2,0,1:T(8,128)} reshape(f32[3,64,1,128]{3,1,2,0:T(8,128)} %get-tuple-element.63) | data formatting | bytes 196608 | tf_op jit(solution)/shard_map/sub | solution.py:92
  76.8 4.4 %multiply_reduce_fusion = f32[3,32,2,32]{3,2,1,0:T(2,128)S(1)} fusion(f32[3,1,32,2,2,32,2]{6,5,4,3,2,0,1:T(8,128)} %sub.321, f32[32,2,2,32,2]{4,3,2,1,0:T(8,128)} %mul.571), kind=kLoop, calls=%fused_computation.2 | loop fusion | flops 43008 | bytes 155648 | tf_op jit(solution)/shard_map/reduce_sum | solution.py:95
  81.2 0.6 copy.216
  81.8 1.0 reshape.878
  82.8 8.4 %sub.319 = f32[3,1,32,2,2,32,2]{6,5,4,3,2,0,1:T(8,128)} reshape(f32[3,64,1,128]{3,1,2,0:T(8,128)} %get-tuple-element.62) | data formatting | bytes 196608 | tf_op jit(solution)/shard_map/sub | solution.py:91
  91.3 4.4 %multiply_reduce_fusion.1 = f32[3,32,2,32]{3,2,1,0:T(2,128)S(1)} fusion(f32[3,1,32,2,2,32,2]{6,5,4,3,2,0,1:T(8,128)} %sub.319, f32[32,2,2,32,2]{4,3,2,1,0:T(8,128)} %mul.568), kind=kLoop, calls=%fused_computation.3 | loop fusion | flops 43008 | bytes 155648 | tf_op jit(solution)/shard_map/reduce_sum | solution.py:95
  96.3 1.0 reshape.877
  97.4 1.0 fusion.109
  99.2 3.0 %fusion.60 = f32[3,64,8,128]{3,1,2,0:T(8,128)S(1)} fusion(f32[3,66,8,128]{3,1,2,0:T(8,128)S(1)} %multiply_add_fusion, f32[3,70,8,128]{3,1,2,0:T(8,128)S(1)} %copy-done.2, f32[3,64,1,128]{3,1,2,0:T(8,128)} %get-tuple-element.64, f32[3,64,7,128]{3,1,2,0:T(8,128)} %get-tuple-element.66, f32[3,64,7,128]{3,1,2,0:T(8,128)} %get-tuple-element.65, ...), kind=kLoop, calls=%fused_computation.88 | loop fusion | flops 4915200 | bytes 8847376 | tf_op jit(solution)/shard_map/sub | solution.py:131
  102.7 51.6 %reshape.875 = f32[3,32,2,4,2,2,32,2]{7,6,5,4,3,2,1,0:T(8,128)} reshape(f32[3,64,8,128]{3,2,1,0:T(8,128)S(1)} %copy.213) | data formatting | bytes 1572864 | tf_op jit(solution)/shard_map/reshape | solution.py:87
  154.3 18.1 %reduce_sum.50 = f32[3,32,4,2,32]{4,3,2,1,0:T(2,128)S(1)} reduce(f32[3,32,2,4,2,2,32,2]{7,6,5,4,3,2,1,0:T(8,128)} %reshape.875, f32[]{:T(128)} %constant.26.clone.1), dimensions={2,4,7}, to_apply=%region_2.3 | reduce | flops 172032 | bytes 884740 | tf_op jit(solution)/shard_map/reduce_sum | solution.py:87
  173.1 0.8 convolution_bitcast_fusion
  173.9 2.2 %copy.217 = f32[16,1,18432]{2,1,0:T(1,128)} copy(f32[16,1,18432]{2,0,1:T(8,128)S(1)} %convolution_bitcast_fusion) | data formatting | bytes 2359296 | tf_op jit(solution)/shard_map/reshape | solution.py:154
  176.1 5.8 %all-to-all-start.1 = ((f32[16,1,18432]{2,1,0:T(1,128)}), f32[16,1,18432]{2,1,0:T(1,128)S(1)}, u32[]{:S(2)}, u32[]{:S(2)}) async-start(f32[16,1,18432]{2,1,0:T(1,128)} %copy.217), calls=%async_computation.1 | async-start | bytes 2359296 | tf_op jit(solution)/shard_map/all_to_all | solution.py:159
  181.9 1.1 reduce.3
  183.1 1.3 copy.219
  184.4 14.8 %all-to-all-done.1 = f32[16,1,18432]{2,1,0:T(1,128)S(1)} async-done(((f32[16,1,18432]{2,1,0:T(1,128)}), f32[16,1,18432]{2,1,0:T(1,128)S(1)}, u32[]{:S(2)}, u32[]{:S(2)}) %all-to-all-start.1) | async-done | bytes 1179680 | tf_op jit(solution)/shard_map/all_to_all | solution.py:159
  199.6 1.7 convolution_bitcast_fusion.1
  (123 shorter events, 11.9 us)
Async XLA Ops:
  0.6 2.8 %copy-start.14 = (f32[3,64,8,128]{3,2,1,0:T(8,128)S(1)}, f32[3,64,8,128]{3,2,1,0:T(8,128)}, u32[]{:S(2)}) copy-start(f32[3,64,8,128]{3,2,1,0:T(8,128)} %param.6) | copy-start | bytes 2359300
  3.4 8.4 %copy-start.15 = (f32[3,64,2,128]{3,2,1,0:T(2,128)S(1)}, f32[3,64,2,128]{3,2,1,0:T(2,128)}, u32[]{:S(2)}) copy-start(f32[3,64,2,128]{3,2,1,0:T(2,128)} %param.7) | copy-start | bytes 589828
  3.4 17.4 %copy-start.24 = (s32[1,2]{1,0:T(1,128)S(1)}, s32[1,2]{1,0:T(1,128)}, u32[]{:S(2)}) copy-start(s32[1,2]{1,0:T(1,128)} %param.11) | copy-start | bytes 28
  3.4 17.6 %copy-start.23 = (s32[1,2]{1,0:T(1,128)S(1)}, s32[1,2]{1,0:T(1,128)}, u32[]{:S(2)}) copy-start(s32[1,2]{1,0:T(1,128)} %param.10) | copy-start | bytes 28
  3.4 27.4 %copy-start = (f32[64,8,128]{2,1,0:T(8,128)S(1)}, f32[64,8,128]{2,1,0:T(8,128)}, u32[]{:S(2)}) copy-start(f32[64,8,128]{2,1,0:T(8,128)} %param.8) | copy-start | bytes 786436
  4.4 46.8 %collective-permute-start.1 = (f32[10,4,8,128]{3,1,2,0:T(4,128)}, f32[10,4,8,128]{3,1,2,0:T(4,128)S(1)}, u32[]{:S(2)}, u32[]{:S(2)}) collective-permute-start(f32[10,4,8,128]{3,1,2,0:T(4,128)} %get-tuple-element.56), channel_id=1, source_target_pairs={{16,0},{32,16},{48,32},{64,48},{80,64},{96,80},{112,96},{128,112},... | collective-permute-start | bytes 491528 | tf_op jit(solution)/shard_map/ppermute | solution.py:27
  5.7 45.5 %collective-permute-start = (f32[10,4,8,128]{3,1,2,0:T(4,128)}, f32[10,4,8,128]{3,1,2,0:T(4,128)S(1)}, u32[]{:S(2)}, u32[]{:S(2)}) collective-permute-start(f32[10,4,8,128]{3,1,2,0:T(4,128)} %get-tuple-element.55), channel_id=1, source_target_pairs={{0,16},{16,32},{32,48},{48,64},{64,80},{80,96},{96,112},{112,128},... | collective-permute-start | bytes 491528 | tf_op jit(solution)/shard_map/ppermute | solution.py:24
  11.9 22.4 %copy-start.9 = (f32[3,64,2,128]{3,1,0,2:T(8,128)}, f32[3,64,2,128]{3,1,0,2:T(8,128)S(1)}, u32[]{:S(2)}) copy-start(f32[3,64,2,128]{3,1,0,2:T(8,128)S(1)} %copy.197) | copy-start | bytes 589828
  12.6 37.5 %collective-permute-start.3 = (f32[3,4,2,128]{3,1,0,2:T(4,128)}, f32[3,4,2,128]{3,1,0,2:T(4,128)}, u32[]{:S(2)}, u32[]{:S(2)}) collective-permute-start(f32[3,4,2,128]{3,1,0,2:T(4,128)} %get-tuple-element.158), channel_id=1, source_target_pairs={{16,0},{32,16},{48,32},{64,48},{80,64},{96,80},{112,96},{128,112},... | collective-permute-start | bytes 36872 | tf_op jit(solution)/shard_map/ppermute | solution.py:27
  13.9 36.3 %collective-permute-start.2 = (f32[3,4,2,128]{3,1,0,2:T(4,128)}, f32[3,4,2,128]{3,1,0,2:T(4,128)}, u32[]{:S(2)}, u32[]{:S(2)}) collective-permute-start(f32[3,4,2,128]{3,1,0,2:T(4,128)} %get-tuple-element.157), channel_id=1, source_target_pairs={{0,16},{16,32},{32,48},{48,64},{64,80},{80,96},{96,112},{112,128},... | collective-permute-start | bytes 36872 | tf_op jit(solution)/shard_map/ppermute | solution.py:24
  21.7 12.6 %copy-start.20 = (s32[2]{0:T(128)}, s32[2]{0:T(128)S(1)}, u32[]{:S(2)}) copy-start(s32[2]{0:T(128)S(1)} %get-tuple-element.173) | copy-start | bytes 28
  22.4 153.7 %all-to-all-start = ((s32[16,1,1]{2,1,0:T(1,128)}), s32[16,1,1]{2,1,0:T(1,128)}, u32[]{:S(2)}, u32[]{:S(2)}) async-start(s32[16,1,1]{2,1,0:T(1,128)} %copy.206), calls=%async_computation | async-start | bytes 16384 | tf_op jit(solution)/shard_map/all_to_all | solution.py:160
  29.0 33.0 %copy-start.16 = (pred[8]{0:T(512)(128)(4,1)}, pred[8]{0:T(512)(128)(4,1)S(1)}, u32[]{:S(2)}) copy-start(pred[8]{0:T(512)(128)(4,1)S(1)} %get-tuple-element.171) | copy-start | bytes 28
  29.0 33.0 %copy-start.18 = (pred[8]{0:T(512)(128)(4,1)}, pred[8]{0:T(512)(128)(4,1)S(1)}, u32[]{:S(2)}) copy-start(pred[8]{0:T(512)(128)(4,1)S(1)} %get-tuple-element.172) | copy-start | bytes 28
  36.8 11.9 %copy-start.8 = (f32[64,8,128]{2,1,0:T(8,128)S(1)}, f32[64,8,128]{2,1,0:T(8,128)}, u32[]{:S(2)}) copy-start(f32[64,8,128]{2,1,0:T(8,128)} %get-tuple-element.139) | copy-start | bytes 786436
  51.2 10.4 %copy-start.6 = (f32[10,4,8,128]{3,1,2,0:T(4,128)}, f32[10,4,8,128]{3,1,2,0:T(4,128)S(1)}, u32[]{:S(2)}) copy-start(f32[10,4,8,128]{3,1,2,0:T(4,128)S(1)} %collective-permute-done.1) | copy-start | bytes 491524
  51.2 10.4 %copy-start.7 = (f32[10,4,8,128]{3,1,2,0:T(4,128)}, f32[10,4,8,128]{3,1,2,0:T(4,128)S(1)}, u32[]{:S(2)}) copy-start(f32[10,4,8,128]{3,1,2,0:T(4,128)S(1)} %collective-permute-done) | copy-start | bytes 491524
  57.1 5.0 %copy-start.1 = (f32[3,70,8,128]{3,1,2,0:T(8,128)}, f32[3,70,8,128]{3,1,2,0:T(8,128)S(1)}, u32[]{:S(2)}) copy-start(f32[3,70,8,128]{3,1,2,0:T(8,128)S(1)} %get-tuple-element.18) | copy-start | bytes 2580484
  64.7 2.9 %copy-start.10 = (f32[3,64,1,128]{3,2,1,0:T(1,128)S(1)}, f32[3,64,1,128]{3,2,1,0:T(1,128)}, u32[]{:S(2)}) copy-start(f32[3,64,1,128]{3,2,1,0:T(1,128)} %get-tuple-element.155) | copy-start | bytes 294916
  64.7 2.9 %copy-start.12 = (f32[3,64,1,128]{3,2,1,0:T(1,128)S(1)}, f32[3,64,1,128]{3,2,1,0:T(1,128)}, u32[]{:S(2)}) copy-start(f32[3,64,1,128]{3,2,1,0:T(1,128)} %get-tuple-element.156) | copy-start | bytes 294916
  97.3 1.2 copy-start.2
  97.3 1.4 copy-start.3
  97.3 1.6 copy-start.4
  97.4 1.9 copy-start.5
  97.4 1.8 copy-start.11
  97.4 1.9 copy-start.13
  97.4 1.9 copy-start.17
  97.4 1.8 copy-start.19
  154.3 18.8 %copy-start.21 = (s32[2]{0:T(128)S(1)}, s32[2]{0:T(128)}, u32[]{:S(2)}) copy-start(s32[2]{0:T(128)} %copy-done.20) | copy-start | bytes 28
  154.3 18.8 %copy-start.22 = (f32[2]{0:T(128)S(1)}, f32[2]{0:T(128)}, u32[]{:S(2)}) copy-start(f32[2]{0:T(128)} %get-tuple-element.174) | copy-start | bytes 28
  176.1 23.1 %all-to-all-start.1 = ((f32[16,1,18432]{2,1,0:T(1,128)}), f32[16,1,18432]{2,1,0:T(1,128)S(1)}, u32[]{:S(2)}, u32[]{:S(2)}) async-start(f32[16,1,18432]{2,1,0:T(1,128)} %copy.217), calls=%async_computation.1 | async-start | bytes 2359296 | tf_op jit(solution)/shard_map/all_to_all | solution.py:159
where the time goes:
time: 205 us; the launch traced here: 201 us
  local copies, waits for them, and re-layouts  109 us (53%)
  other arithmetic  45.9 us (22%)
  starting transfers between devices  28 us (14%)
  waiting for transfers between devices  14.8 us (7%)
  matrix products  2.47 us (1%)
    reshape x1, local copies, waits for them, and re-layouts, patch_data(): residual.reshape(3, groups, half, 2, CY // 2, 2, P_SIZE, half, 2)  51.6 us
    reduce_sum x1, other arithmetic, patch_data(): residual.reshape(3, groups, half, 2, CY // 2, 2, P_SIZE, half, 2)  18.1 us
    all_to_all x1, waiting for transfers between devices, on_device(): lax.all_to_all(buffer, 'wide', split_axis=0, concat_axis=0, tiled=True)  14.8 us
    ppermute x2, starting transfers between devices, with_halo(): lax.ppermute(lax.slice_in_dim(block, block.shape[dim] - width, None, axis...  13.1 us
    reduce_sum x2, other arithmetic, faces(): flux.reshape(3, groups, half, 2, P_SIZE, half, 2).mean(axis=(3, 6))  8.72 us
    sub x1, local copies, waits for them, and re-layouts, patch_data(): smoothed[:, :, 0, :] - coarse_ghost[:, :, 0, :]  8.42 us
    sub x1, local copies, waits for them, and re-layouts, patch_data(): coarse_ghost[:, :, 1, :] - smoothed[:, :, -1, :]  8.41 us
    all_to_all x1, starting transfers between devices, on_device(): lax.all_to_all(labels, 'wide', split_axis=0, concat_axis=0, tiled=True)  6.56 us
  transfers between devices with their start and end apart: 6, of which 1 were waited for; matrix products, arithmetic and copies ran while one was open for 75% of the time, Pallas kernels for 0%

commit v1 on v0

v1 whole, which is shorter than its diff:
```python
import functools

import jax
import jax.numpy as jnp
from jax import lax
from jax.experimental import pallas as pl
from jax.experimental.pallas import tpu as pltpu
from jax.sharding import PartitionSpec as P

MESH = pl.DeviceIdType.MESH
F32 = jnp.float32

NX = 64
M = 4
EX = NX + 2 * M
KAPPA = 1.0
OMEGA = 0.8
CP_DEV = 16

CHUNKS = (
    (0, 40, ((0, 2, 8), (8, 10, 8), (16, 18, 8), (24, 26, 4), (28, 33, 6), (34, 41, 6))),
    (120, 8, ((0, 0, 2), (2, 30, 2), (4, 32, 1), (5, 39, 1), (6, 40, 1), (7, 47, 1))),
)


def step_kernel(
    n_grp, n_wide,
    mask_ref, owner_ref, vel_hbm, ghost_hbm, visc_hbm, stress_hbm,
    newvel_hbm, recv_hbm, labels_hbm,
    u0, st, vi, gh, fe, fw, fn, fs, fu, fd, ww, dd, ve, sp, gv, u1, u2, u3, rs, fl,
    lhs, mat, slots, lab,
    in_sem, halo_send, halo_recv, lab_send, lab_recv, pay_send, pay_recv, out_sem,
):
    g = lax.axis_index("grp")
    wd = lax.axis_index("wide")
    up = lax.rem(g + 1, n_grp)
    down = lax.rem(g + n_grp - 1, n_grp)

    loads = [
        pltpu.make_async_copy(vel_hbm, u0.at[:, pl.ds(M, NX)], in_sem.at[0]),
        pltpu.make_async_copy(stress_hbm, st.at[:, pl.ds(M, NX)], in_sem.at[1]),
        pltpu.make_async_copy(visc_hbm, vi.at[pl.ds(M, NX)], in_sem.at[2]),
        pltpu.make_async_copy(ghost_hbm, gh.at[:, pl.ds(M, NX)], in_sem.at[3]),
    ]
    for copy in loads:
        copy.start()

    barrier = pltpu.get_barrier_semaphore()
    for other in (up, down):
        pl.semaphore_signal(barrier, inc=1, device_id=(other, wd), device_id_type=MESH)
    for d in range(1, n_wide):
        pl.semaphore_signal(
            barrier, inc=1, device_id=(g, lax.rem(wd + d, n_wide)), device_id_type=MESH
        )
    lane = lax.broadcasted_iota(jnp.int32, (1, 128), 1)
    lab[...] = jnp.where(lane == 0, owner_ref[0, 0], owner_ref[0, 1])
    pl.semaphore_wait(barrier, n_wide + 1)

    halos = []
    for side, (other, src, dst) in enumerate(((up, NX - M, 0), (down, 0, M + NX))):
        pairs = (
            (vel_hbm.at[:, pl.ds(src, M)], u0.at[:, pl.ds(dst, M)]),
            (visc_hbm.at[pl.ds(src, M)], vi.at[pl.ds(dst, M)]),
            (stress_hbm.at[:, pl.ds(src, M)], st.at[:, pl.ds(dst, M)]),
            (ghost_hbm.at[:, pl.ds(src, M)], gh.at[:, pl.ds(dst, M)]),
        )
        for i, (s, t) in enumerate(pairs):
            halos.append(
                pltpu.make_async_remote_copy(
                    src_ref=s, dst_ref=t,
                    send_sem=halo_send.at[side, i], recv_sem=halo_recv.at[side, i],
                    device_id=(other, wd), device_id_type=MESH,
                )
            )
    for copy in halos:
        copy.start()

    def label_copy(d):
        return pltpu.make_async_remote_copy(
            src_ref=lab, dst_ref=labels_hbm.at[d],
            send_sem=lab_send.at[d], recv_sem=lab_recv.at[d],
            device_id=(g, lax.rem(wd + d, n_wide)), device_id_type=MESH,
        )

    for d in range(1, n_wide):
        label_copy(d).start()
    own_label = pltpu.make_async_copy(lab, labels_hbm.at[0], out_sem.at[1])
    own_label.start()

    row = lax.broadcasted_iota(jnp.int32, (512, 256), 0)
    col = lax.broadcasted_iota(jnp.int32, (512, 256), 1)
    same_q = lax.shift_right_logical(row, 7) == (lax.shift_right_logical(col, 5) & 3)
    z_pair = lax.shift_right_logical(row & 127, 1)
    z_want = lax.shift_right_logical(col, 7) * 32 + (col & 31)
    mat[...] = jnp.where(same_q & (z_pair == z_want), 1.0, 0.0).astype(jnp.bfloat16)

    ypos = lax.broadcasted_iota(jnp.int32, (1, 8, 128), 1)
    not_last = ypos < 7
    not_first = ypos > 0

    def y_up(a):
        return pltpu.roll(a, 7, 1)

    def y_dn(a):
        return pltpu.roll(a, 1, 1)

    def z_up(a):
        return pltpu.roll(a, 127, 2)

    def z_dn(a):
        return pltpu.roll(a, 1, 2)

    def prep(lo, n, inside=None):
        here, after, before = pl.ds(lo, n), pl.ds(lo + 1, n), pl.ds(lo - 1, n)
        v = vi[here]
        f_e = 0.5 * (v + vi[after])
        f_w = 0.5 * (v + vi[before])
        f_n = jnp.where(not_last, 0.5 * (v + y_up(v)), 0.0)
        f_s = y_dn(f_n)
        f_u = 0.5 * (v + z_up(v))
        f_d = z_dn(f_u)
        v_edge = jnp.where(not_last & not_first, 0.0, v)
        diag = KAPPA + f_e + f_w + f_n + f_s + f_u + f_d + v_edge
        weight = OMEGA / diag
        if inside is not None:
            weight = weight * inside
        fe[here], fw[here], fn[here], fs[here], fu[here], fd[here] = f_e, f_w, f_n, f_s, f_u, f_d
        ww[here], dd[here] = weight, diag
        ve[here] = v_edge

        def d_x(c):
            return st[c, after] - st[c, before]

        def d_y(a):
            return jnp.where(not_last, y_up(a), 0.0) - jnp.where(not_first, y_dn(a), 0.0)

        def d_z(a):
            return z_up(a) - z_dn(a)

        ghost_edges = []
        for c in range(3):
            low = jnp.broadcast_to(gh[c, here, 0:1, :], (n, 8, 128))
            high = jnp.broadcast_to(gh[c, here, 1:2, :], (n, 8, 128))
            edge = jnp.where(not_first, jnp.where(not_last, 0.0, high), low)
            gv[c, here] = edge
            ghost_edges.append(v_edge * edge)
        sxy, sxz, syz = st[3, here], st[4, here], st[5, here]
        sp[0, here] = u0[0, here] + 0.5 * (d_x(0) + d_y(sxy) + d_z(sxz)) + ghost_edges[0]
        sp[1, here] = u0[1, here] + 0.5 * (d_x(3) + d_y(st[1, here]) + d_z(syz)) + ghost_edges[1]
        sp[2, here] = u0[2, here] + 0.5 * (d_x(4) + d_y(syz) + d_z(st[2, here])) + ghost_edges[2]

    def flow(src, lo, n):
        here, after, before = pl.ds(lo, n), pl.ds(lo + 1, n), pl.ds(lo - 1, n)
        f_e, f_w, f_n, f_s, f_u, f_d = fe[here], fw[here], fn[here], fs[here], fu[here], fd[here]
        for c in range(3):
            u = src[c, here]
            total = (
                (sp[c, here] + f_e * src[c, after] + f_w * src[c, before])
                + (f_n * y_up(u) + f_s * y_dn(u))
                + (f_u * z_up(u) + f_d * z_dn(u))
            )
            yield c, u, total

    def sweep(src, dst, lo, n):
        here = pl.ds(lo, n)
        weight = ww[here]
        for c, u, total in flow(src, lo, n):
            dst[c, here] = (1.0 - OMEGA) * u + weight * total

    def restrict(lo, n):
        here = pl.ds(lo, n)
        diag, v_edge = dd[here], ve[here]
        half = n // 2
        pairs = pl.ds(pl.multiple_of((lo - M) * 4, 8), half * 8)
        for c, u, total in flow(u3, lo, n):
            res = (total - diag * u).reshape(half, 2, 8, 128)
            res = res[:, 0] + res[:, 1]
            res = res + y_up(res)
            rs[c, pairs] = res.reshape(half * 8, 128)
            flux = (v_edge * (u - gv[c, here])).reshape(half, 2, 8, 128)
            fl[c, pairs] = (flux[:, 0] + flux[:, 1]).reshape(half * 8, 128)

    def over(fn_, lo, hi, n):
        count = (hi - lo) // n

        def body(i, carry):
            fn_(lo + i * n, n)
            return carry

        lax.fori_loop(0, count, body, 0)
        if (hi - lo) % n:
            fn_(lo + count * n, (hi - lo) % n)

    mask0 = mask_ref[0, 0].astype(F32)
    mask1 = mask_ref[0, 1].astype(F32)
    target0 = owner_ref[0, 0] // CP_DEV
    target1 = owner_ref[0, 1] // CP_DEV

    def payload_copy(chunk, d):
        base, rows, _ = CHUNKS[chunk]
        return pltpu.make_async_remote_copy(
            src_ref=slots.at[d, pl.ds(base, 3 * rows)],
            dst_ref=recv_hbm.at[d, pl.ds(base, 3 * rows)],
            send_sem=pay_send.at[chunk, d], recv_sem=pay_recv.at[chunk, d],
            device_id=(g, lax.rem(wd + d, n_wide)), device_id_type=MESH,
        )

    def own_copy(chunk):
        base, rows, _ = CHUNKS[chunk]
        return pltpu.make_async_copy(
            slots.at[0, pl.ds(base, 3 * rows)], recv_hbm.at[0, pl.ds(base, 3 * rows)],
            out_sem.at[2 + chunk],
        )

    def send(chunk):
        base, rows, segments = CHUNKS[chunk]
        for c in range(3):
            for at, tile, count in segments:
                for q in range(4):
                    if tile < 32:
                        piece = rs[c, pl.ds(tile * 8 + 2 * q, count, stride=8), :] * 0.125
                    else:
                        fr, y, sign = (tile - 32, 0, 0.25) if tile < 40 else (tile - 40, 7, -0.25)
                        piece = fl[c, pl.ds(fr * 32 + q * 8 + y, count, stride=32), :] * sign
                    lhs[pl.ds(c * rows + at, count), pl.ds(q * 128, 128)] = piece
        full = lhs[pl.ds(0, 3 * rows), :]
        high = full.astype(jnp.bfloat16)
        low = (full - high.astype(F32)).astype(jnp.bfloat16)
        m = mat[...]
        out = jnp.dot(high, m, preferred_element_type=F32) + jnp.dot(
            low, m, preferred_element_type=F32
        )
        p0 = out[:, :128] * mask0
        p1 = out[:, 128:] * mask1
        for d in range(n_wide):
            t = lax.rem(wd + d, n_wide)
            s0 = jnp.where(target0 == t, 1.0, 0.0)
            s1 = jnp.where(target1 == t, 1.0, 0.0)
            slots[d, pl.ds(base, 3 * rows), :] = p0 * s0 + p1 * s1
            if d:
                payload_copy(chunk, d).start()
            else:
                own_copy(chunk).start()

    for copy in loads:
        copy.wait()

    over(prep, M + 1, M + NX - 1, 4)
    over(functools.partial(sweep, u0, u1), M + 1, M + NX - 1, 4)
    over(functools.partial(sweep, u1, u2), M + 2, M + NX - 2, 4)
    over(functools.partial(sweep, u2, u3), M + 3, M + NX - 3, 4)
    over(restrict, M + 4, M + NX - 4, 4)
    send(0)

    for copy in halos:
        copy.wait()
    inside_low = jnp.where(g > 0, 1.0, 0.0)
    inside_high = jnp.where(g < n_grp - 1, 1.0, 0.0)
    for at, inside in ((0, inside_low), (M + NX, inside_high)):
        here = pl.ds(at, M)
        u0[:, here] = u0[:, here] * inside
        st[:, here] = st[:, here] * inside
        vi[here] = vi[here] * inside
    prep(1, 3, inside_low)
    prep(M, 1)
    prep(M + NX - 1, 1)
    prep(M + NX, 3, inside_high)
    for src, dst, shift in ((u0, u1, 1), (u1, u2, 2), (u2, u3, 3)):
        sweep(src, dst, shift, 4)
        sweep(src, dst, EX - 4 - shift, 4)
    store = pltpu.make_async_copy(u3.at[:, pl.ds(M, NX)], newvel_hbm, out_sem.at[0])
    store.start()
    restrict(M, 4)
    restrict(M + NX - 4, 4)
    send(1)

    for d in range(1, n_wide):
        label_copy(d).wait()
        for chunk in range(2):
            payload_copy(chunk, d).wait()
    own_label.wait()
    own_copy(0).wait()
    own_copy(1).wait()
    store.wait()


def sum_kernel(n_wide, labels_ref, vel_hbm, recv_hbm, newvel_hbm, out_ref, recv, sems):
    me = lax.axis_index("wide")
    move = pltpu.make_async_copy(vel_hbm, newvel_hbm, sems.at[0])
    fetch = pltpu.make_async_copy(recv_hbm, recv, sems.at[1])
    fetch.start()
    move.start()
    out_ref[...] = jnp.zeros_like(out_ref)
    fetch.wait()
    for d in range(n_wide):
        first, second = labels_ref[d, 0, 0], labels_ref[d, 0, 1]
        hit0 = first // CP_DEV == me
        hit1 = second // CP_DEV == me
        index = jnp.where(hit0, first, second) % CP_DEV

        @pl.when(hit0 | hit1)
        def _():
            start = (index // 8) * 384 + index % 8
            for base, rows, segments in CHUNKS:
                for c in range(3):
                    for at, tile, count in segments:
                        where = pl.ds(start + c * 768 + tile * 8, count, stride=8)
                        out_ref[where, :] = (
                            out_ref[where, :] + recv[d, pl.ds(base + c * rows + at, count), :]
                        )

    move.wait()


def on_device(velocity, coarse_ghost, viscosity, stress, patch_mask, coarse_owner):
    n_grp, n_wide = lax.axis_size("grp"), lax.axis_size("wide")
    hbm = pl.BlockSpec(memory_space=pltpu.HBM)
    smem = pl.BlockSpec(memory_space=pltpu.SMEM)
    scalar_field = pltpu.VMEM((EX, 8, 128), F32)
    field = pltpu.VMEM((3, EX, 8, 128), F32)
    new_velocity, received, labels = pl.pallas_call(
        functools.partial(step_kernel, n_grp, n_wide),
        out_shape=(
            jax.ShapeDtypeStruct((3, NX, 8, 128), F32),
            jax.ShapeDtypeStruct((n_wide, 144, 128), F32),
            jax.ShapeDtypeStruct((n_wide, 1, 128), jnp.int32),
        ),
        in_specs=[smem, smem, hbm, hbm, hbm, hbm],
        out_specs=(hbm, hbm, hbm),
        scratch_shapes=[
            field, pltpu.VMEM((6, EX, 8, 128), F32), scalar_field, pltpu.VMEM((3, EX, 2, 128), F32),
            *[scalar_field] * 9,
            field, field, field, field, field,
            pltpu.VMEM((3, 256, 128), F32), pltpu.VMEM((3, 256, 128), F32),
            pltpu.VMEM((120, 512), F32), pltpu.VMEM((512, 256), jnp.bfloat16),
            pltpu.VMEM((n_wide, 144, 128), F32), pltpu.VMEM((1, 128), jnp.int32),
            pltpu.SemaphoreType.DMA((4,)),
            pltpu.SemaphoreType.DMA((2, 4)), pltpu.SemaphoreType.DMA((2, 4)),
            pltpu.SemaphoreType.DMA((n_wide,)), pltpu.SemaphoreType.DMA((n_wide,)),
            pltpu.SemaphoreType.DMA((2, n_wide)), pltpu.SemaphoreType.DMA((2, n_wide)),
            pltpu.SemaphoreType.DMA((4,)),
        ],
        compiler_params=pltpu.CompilerParams(
            collective_id=0, has_side_effects=True, vmem_limit_bytes=40 << 20
        ),
        name="smooth_and_send",
    )(patch_mask, coarse_owner, velocity, coarse_ghost, viscosity, stress)
    new_velocity, coarse = pl.pallas_call(
        functools.partial(sum_kernel, n_wide),
        out_shape=(
            jax.ShapeDtypeStruct((3, NX, 8, 128), F32),
            jax.ShapeDtypeStruct((2304, 128), F32),
        ),
        in_specs=[smem, hbm, hbm],
        out_specs=(hbm, pl.BlockSpec(memory_space=pltpu.VMEM)),
        scratch_shapes=[pltpu.VMEM((n_wide, 144, 128), F32), pltpu.SemaphoreType.DMA((2,))],
        compiler_params=pltpu.CompilerParams(vmem_limit_bytes=40 << 20),
        name="sum_on_owners",
    )(labels, new_velocity, received)
    coarse = coarse.reshape(3, 2, 48, 8, 128).transpose(1, 3, 0, 2, 4)
    return new_velocity, coarse.reshape(1, CP_DEV, 3, 48 * 128)


def solution(mesh):
    in_specs = (
        P(None, "grp", "wide", None),
        P(None, "grp", "wide", None),
        P("grp", "wide", None),
        P(None, "grp", "wide", None),
        P("grp", "wide"),
        P("grp", "wide"),
    )
    out_specs = (P(None, "grp", "wide", None), P("grp", "wide", None, None))
    return jax.shard_map(
        on_device, mesh=mesh, in_specs=in_specs, out_specs=out_specs, check_vma=False
    )
```

time: 205 us -> 46 us (0.22); the launches traced: 201 us -> 45.8 us
  local copies, waits for them, and re-layouts: 109 us -> 5.72 us
  other arithmetic: 45.9 us -> 0 us
  Pallas kernels: 0 us -> 39.4 us
  starting transfers between devices: 28 us -> 0 us
  waiting for transfers between devices: 14.8 us -> 0 us
  matrix products: 2.47 us -> 0 us
    reshape x5 -> x0, local copies, waits for them, and re-layouts: 56.1 us -> none  [the longest x1 51.6 us: patch_data(): residual.reshape(3, groups, half, 2, CY // 2, 2, P_SIZE, half, 2)]
    pallas_call x0 -> x2, Pallas kernels: none -> 39.4 us  [the longest x1 36.6 us: on_device(): pl.pallas_call(functools.partial(step_kernel, n_grp, n_wide), out_shape=(...]
    reduce_sum x5 -> x0, other arithmetic: 27.1 us -> none  [the longest x1 18.1 us: patch_data(): residual.reshape(3, groups, half, 2, CY // 2, 2, P_SIZE, half, 2)]
    sub x4 -> x0, local copies, waits for them, and re-layouts: 18 us -> none  [the longest x1 8.42 us: patch_data(): smoothed[:, :, 0, :] - coarse_ghost[:, :, 0, :]]
    ppermute x4 -> x0, starting transfers between devices: 15.7 us -> none  [the longest x2 13.1 us: with_halo(): lax.ppermute(lax.slice_in_dim(block, block.shape[dim] - width, None, axis...]
    all_to_all x2 -> x0, waiting for transfers between devices: 14.8 us -> none  [the longest x1 14.8 us: on_device(): lax.all_to_all(buffer, 'wide', split_axis=0, concat_axis=0, tiled=True)]
    mul x6 -> x0, local copies, waits for them, and re-layouts: 13.3 us -> none  [the longest x1 4.23 us: patch_data(): viscosity[:, 0, :] * (smoothed[:, :, 0, :] - coarse_ghost[:, :, 0, :])]
    slice x24 -> x0, local copies, waits for them, and re-layouts: 12.4 us -> none  [the longest x2 2.92 us: apply_operator(): jnp.roll(interior, 1, axis=3)]
  transfers between devices with their start and end apart: 6 -> 0, of which waited for: 1 -> 0; matrix products, arithmetic and copies ran while one was open for 75% -> 0% of each run, Pallas kernels for 0% -> 0%
where the time goes in v1:
time: 46 us; the launch traced here: 45.8 us
  Pallas kernels  39.4 us (86%)
  local copies, waits for them, and re-layouts  5.72 us (12%)
  between operations  0.65 us (1%)
    pallas_call x1, Pallas kernels, on_device(): pl.pallas_call(functools.partial(step_kernel, n_grp, n_wide), out_shape=(...  36.6 us
    unnamed x12, local copies, waits for them, and re-layouts  5.72 us
    pallas_call x1, Pallas kernels, on_device(): pl.pallas_call(functools.partial(sum_kernel, n_wide), out_shape=(jax.Shap...  2.82 us

profile of v1, /device:TPU:1, one launch (start us, length us, event | category | flops | bytes accessed | tf_op | source)
XLA Modules:
  0.0 45.8 jit_solution(2642342861678528238)
XLA Ops:
  0.6 0.0 copy-start
  0.6 1.4 %copy-done = f32[6,64,8,128]{3,2,1,0:T(8,128)S(1)} copy-done((f32[6,64,8,128]{3,2,1,0:T(8,128)S(1)}, f32[6,64,8,128]{3,2,1,0:T(8,128)}, u32[]{:S(2)}) %copy-start) | copy-done | bytes 1572888
  2.0 0.0 copy-start.1
  2.0 1.1 %copy-done.1 = f32[3,64,8,128]{3,2,1,0:T(8,128)S(1)} copy-done((f32[3,64,8,128]{3,2,1,0:T(8,128)S(1)}, f32[3,64,8,128]{3,2,1,0:T(8,128)}, u32[]{:S(2)}) %copy-start.1) | copy-done | bytes 786456
  3.2 0.0 copy-start.2
  3.2 0.9 %copy-done.2 = f32[64,8,128]{2,1,0:T(8,128)S(1)} copy-done((f32[64,8,128]{2,1,0:T(8,128)S(1)}, f32[64,8,128]{2,1,0:T(8,128)}, u32[]{:S(2)}) %copy-start.2) | copy-done | bytes 262168
  4.1 0.0 copy-start.3
  4.1 0.9 %copy-done.3 = f32[3,64,2,128]{3,2,1,0:T(2,128)S(1)} copy-done((f32[3,64,2,128]{3,2,1,0:T(2,128)S(1)}, f32[3,64,2,128]{3,2,1,0:T(2,128)}, u32[]{:S(2)}) %copy-start.3) | copy-done | bytes 196632
  5.1 0.0 copy-start.4
  5.1 0.7 %copy-done.4 = s32[1,2]{1,0:T(1,128)S(1)} copy-done((s32[1,2]{1,0:T(1,128)S(1)}, s32[1,2]{1,0:T(1,128)}, u32[]{:S(2)}) %copy-start.4) | copy-done | bytes 32
  5.7 0.0 copy-start.5
  5.7 0.7 %copy-done.5 = s32[1,2]{1,0:T(1,128)S(1)} copy-done((s32[1,2]{1,0:T(1,128)S(1)}, s32[1,2]{1,0:T(1,128)}, u32[]{:S(2)}) %copy-start.5) | copy-done | bytes 32
  6.4 36.6 %smooth_and_send.1 = (f32[3,64,8,128]{3,2,1,0:T(8,128)S(1)}, f32[16,144,128]{2,1,0:T(8,128)S(1)}, s32[16,1,128]{2,1,0:T(1,128)S(1)}) custom-call(s32[1,2]{1,0:T(1,128)S(1)} %copy-done.4, s32[1,2]{1,0:T(1,128)S(1)} %copy-done.5, f32[3,64,8,128]{3,2,1,0:T(8,128)S(1)} %copy-done.1, f32[3,64,2,128]{3,2,1,0:T(2,128)S(1)} %copy-done.3, ...), custom_call_target="tpu_custom_call" | custom-call | tf_op jit(solution)/shard_map/smooth_and_send/pallas_call | solution.py:321
  42.9 2.8 %sum_on_owners.1 = (f32[3,64,8,128]{3,2,1,0:T(8,128)}, f32[2304,128]{1,0:T(8,128)}) custom-call(s32[16,1,128]{2,1,0:T(1,128)S(1)} %get-tuple-element.7.labels_ref, f32[3,64,8,128]{3,2,1,0:T(8,128)S(1)} %get-tuple-element.8.vel_hbm, f32[16,144,128]{2,1,0:T(8,128)S(1)} %get-tuple-element.9.recv_hbm), custom_call_target="tpu_custom_call" | custom-call | tf_op jit(solution)/shard_map/sum_on_owners/pallas_call | solution.py:348
Async XLA Ops:
  0.6 1.4 %copy-start = (f32[6,64,8,128]{3,2,1,0:T(8,128)S(1)}, f32[6,64,8,128]{3,2,1,0:T(8,128)}, u32[]{:S(2)}) copy-start(f32[6,64,8,128]{3,2,1,0:T(8,128)} %stress_hbm.1) | copy-start | bytes 4718596
  2.0 1.1 %copy-start.1 = (f32[3,64,8,128]{3,2,1,0:T(8,128)S(1)}, f32[3,64,8,128]{3,2,1,0:T(8,128)}, u32[]{:S(2)}) copy-start(f32[3,64,8,128]{3,2,1,0:T(8,128)} %vel_hbm.1) | copy-start | bytes 2359300
  3.2 0.9 %copy-start.2 = (f32[64,8,128]{2,1,0:T(8,128)S(1)}, f32[64,8,128]{2,1,0:T(8,128)}, u32[]{:S(2)}) copy-start(f32[64,8,128]{2,1,0:T(8,128)} %visc_hbm.1) | copy-start | bytes 786436
  4.1 0.9 %copy-start.3 = (f32[3,64,2,128]{3,2,1,0:T(2,128)S(1)}, f32[3,64,2,128]{3,2,1,0:T(2,128)}, u32[]{:S(2)}) copy-start(f32[3,64,2,128]{3,2,1,0:T(2,128)} %ghost_hbm.1) | copy-start | bytes 589828
  5.1 0.7 %copy-start.4 = (s32[1,2]{1,0:T(1,128)S(1)}, s32[1,2]{1,0:T(1,128)}, u32[]{:S(2)}) copy-start(s32[1,2]{1,0:T(1,128)} %mask_ref.1) | copy-start | bytes 28
  5.7 0.7 %copy-start.5 = (s32[1,2]{1,0:T(1,128)S(1)}, s32[1,2]{1,0:T(1,128)}, u32[]{:S(2)}) copy-start(s32[1,2]{1,0:T(1,128)} %owner_ref.1) | copy-start | bytes 28

commit v2 on v1

v2 whole, which is shorter than its diff:
```python
import functools

import jax
import jax.numpy as jnp
from jax import lax
from jax.experimental import pallas as pl
from jax.experimental.pallas import tpu as pltpu
from jax.sharding import PartitionSpec as P

MESH = pl.DeviceIdType.MESH
F32 = jnp.float32

NX = 64
M = 4
EX = NX + 2 * M
KAPPA = 1.0
OMEGA = 0.8
CP_DEV = 16
N_WIDE = 16
DX_COMPS = (0, 3, 4)

MAIN = (
    (0, 8, ((0, 2, 6), (6, 33, 1), (7, 41, 1))),
    (24, 16, ((0, 8, 8), (8, 16, 4), (12, 34, 2), (14, 42, 2))),
    (72, 16, ((0, 20, 8), (8, 28, 2), (10, 36, 3), (13, 44, 3))),
)
EDGE = (0, 8, ((0, 0, 2), (2, 30, 2), (4, 32, 1), (5, 39, 1), (6, 40, 1), (7, 47, 1)))


def step_kernel(
    n_grp,
    mask_hbm, owner_hbm, vel_hbm, ghost_hbm, visc_hbm, stress_hbm,
    newvel_hbm, main_hbm, edge_hbm, labels_hbm,
    u0, st, sx, vi, gh, fe, fw, fn, fs, fu, fd, ww, dd, ve, sp, gv, u1, u2, u3, rs, fl,
    lhs, mat, own, slots, lab, mask_ref, owner_ref,
    in_sem, halo_send, halo_recv, lab_send, lab_recv, edge_send, edge_recv, main_send, main_recv,
    out_sem,
):
    g = lax.axis_index("grp")
    wd = lax.axis_index("wide")
    up = lax.rem(g + 1, n_grp)
    down = lax.rem(g + n_grp - 1, n_grp)
    y, x, core = wd // 4, (wd // 2) % 2, wd % 2

    def wide_at(dy, fx, fc):
        return (
            ((y + dy) % 4) * 4
            + (1 - x if fx else x) * 2
            + (1 - core if fc else core)
        )

    others = [(dy, fx, fc) for dy in (2, 1, 3, 0) for fx in (1, 0) for fc in (0, 1)]
    others.remove((0, 0, 0))

    def slot_of(dy, fx, fc):
        return ((dy % 4) * 2 + fx) * 2 + fc

    loads = [
        pltpu.make_async_copy(visc_hbm, vi.at[pl.ds(M, NX)], in_sem.at[2]),
        pltpu.make_async_copy(stress_hbm, st.at[:, pl.ds(1, NX)], in_sem.at[1]),
        pltpu.make_async_copy(vel_hbm, u0.at[:, pl.ds(M, NX)], in_sem.at[0]),
        pltpu.make_async_copy(ghost_hbm, gh, in_sem.at[3]),
        pltpu.make_async_copy(owner_hbm, owner_ref, in_sem.at[4]),
        pltpu.make_async_copy(mask_hbm, mask_ref, in_sem.at[5]),
    ]
    for copy in loads:
        copy.start()

    barrier = pltpu.get_barrier_semaphore()
    for other in (up, down):
        pl.semaphore_signal(barrier, inc=1, device_id=(other, wd), device_id_type=MESH)
    for off in others:
        pl.semaphore_signal(barrier, inc=1, device_id=(g, wide_at(*off)), device_id_type=MESH)

    row = lax.broadcasted_iota(jnp.int32, (512, 256), 0)
    col = lax.broadcasted_iota(jnp.int32, (512, 256), 1)
    same_q = lax.shift_right_logical(row, 7) == (lax.shift_right_logical(col, 5) & 3)
    z_pair = lax.shift_right_logical(row & 127, 1)
    z_want = lax.shift_right_logical(col, 7) * 32 + (col & 31)
    mat[...] = jnp.where(same_q & (z_pair == z_want), 1.0, 0.0).astype(jnp.bfloat16)
    for comp in DX_COMPS:
        st[comp, 0] = jnp.zeros((8, 128), F32)
        st[comp, NX + 1] = jnp.zeros((8, 128), F32)

    ypos = lax.broadcasted_iota(jnp.int32, (1, 8, 128), 1)
    not_last = ypos < 7
    not_first = ypos > 0

    def y_up(a):
        return pltpu.roll(a, 7, 1)

    def y_dn(a):
        return pltpu.roll(a, 1, 1)

    def z_up(a):
        return pltpu.roll(a, 127, 2)

    def z_dn(a):
        return pltpu.roll(a, 1, 2)

    def faces(lo, n, inside=None):
        here, after, before = pl.ds(lo, n), pl.ds(lo + 1, n), pl.ds(lo - 1, n)
        v = vi[here]
        f_e = 0.5 * (v + vi[after])
        f_w = 0.5 * (v + vi[before])
        f_n = jnp.where(not_last, 0.5 * (v + y_up(v)), 0.0)
        f_s = y_dn(f_n)
        f_u = 0.5 * (v + z_up(v))
        f_d = z_dn(f_u)
        v_edge = jnp.where(not_last & not_first, 0.0, v)
        diag = KAPPA + f_e + f_w + f_n + f_s + f_u + f_d + v_edge
        weight = OMEGA / diag
        if inside is not None:
            weight = weight * inside
        fe[here], fw[here], fn[here], fs[here], fu[here], fd[here] = f_e, f_w, f_n, f_s, f_u, f_d
        ww[here], dd[here] = weight, diag

    def force(lo, n):
        here, own_rows = pl.ds(lo, n), pl.ds(lo - M, n)
        mid, after, before = pl.ds(lo - 3, n), pl.ds(lo - 2, n), pl.ds(lo - 4, n)
        v_edge = jnp.where(not_last & not_first, 0.0, vi[here])
        ve[here] = v_edge

        def d_x(c):
            return st[c, after] - st[c, before]

        def d_y(a):
            return jnp.where(not_last, y_up(a), 0.0) - jnp.where(not_first, y_dn(a), 0.0)

        def d_z(a):
            return z_up(a) - z_dn(a)

        sxy, sxz, syz = st[3, mid], st[4, mid], st[5, mid]
        slopes = (
            d_x(0) + d_y(sxy) + d_z(sxz),
            d_x(3) + d_y(st[1, mid]) + d_z(syz),
            d_x(4) + d_y(syz) + d_z(st[2, mid]),
        )
        for c in range(3):
            low = jnp.broadcast_to(gh[c, own_rows, 0:1, :], (n, 8, 128))
            high = jnp.broadcast_to(gh[c, own_rows, 1:2, :], (n, 8, 128))
            edge = jnp.where(not_first, jnp.where(not_last, 0.0, high), low)
            gv[c, here] = edge
            sp[c, here] = KAPPA * u0[c, here] + 0.5 * slopes[c] + v_edge * edge

    def flow(src, lo, n):
        here, after, before = pl.ds(lo, n), pl.ds(lo + 1, n), pl.ds(lo - 1, n)
        f_e, f_w, f_n, f_s, f_u, f_d = fe[here], fw[here], fn[here], fs[here], fu[here], fd[here]
        for c in range(3):
            u = src[c, here]
            total = (
                (sp[c, here] + f_e * src[c, after] + f_w * src[c, before])
                + (f_n * y_up(u) + f_s * y_dn(u))
                + (f_u * z_up(u) + f_d * z_dn(u))
            )
            yield c, u, total

    def sweep(src, dst, lo, n):
        here = pl.ds(lo, n)
        weight = ww[here]
        for c, u, total in flow(src, lo, n):
            dst[c, here] = (1.0 - OMEGA) * u + weight * total

    def restrict(lo, n):
        here = pl.ds(lo, n)
        diag, v_edge = dd[here], ve[here]
        half = n // 2
        pairs = pl.ds((lo - M) * 4, half * 8)
        for c, u, total in flow(u3, lo, n):
            res = (total - diag * u).reshape(half, 2, 8, 128)
            res = res[:, 0] + res[:, 1]
            res = res + y_up(res)
            rs[c, pairs] = res.reshape(half * 8, 128)
            flux = (v_edge * (u - gv[c, here])).reshape(half, 2, 8, 128)
            fl[c, pairs] = (flux[:, 0] + flux[:, 1]).reshape(half * 8, 128)

    def means(chunk):
        base, rows, pieces = chunk
        for c in range(3):
            for at, tile, count in pieces:
                for q in range(4):
                    if tile < 32:
                        piece = rs[c, pl.ds(tile * 8 + 2 * q, count, stride=8), :] * 0.125
                    else:
                        fr, yy, sign = (tile - 32, 0, 0.25) if tile < 40 else (tile - 40, 7, -0.25)
                        piece = fl[c, pl.ds(fr * 32 + q * 8 + yy, count, stride=32), :] * sign
                    lhs[pl.ds(c * rows + at, count), pl.ds(q * 128, 128)] = piece
        full = lhs[pl.ds(0, 3 * rows), :]
        high = full.astype(jnp.bfloat16)
        low = (full - high.astype(F32)).astype(jnp.bfloat16)
        m = mat[...]
        out = jnp.dot(high, m, preferred_element_type=F32) + jnp.dot(
            low, m, preferred_element_type=F32
        )
        return out[:, :128] * mask0, out[:, 128:] * mask1

    def main_copy(k, which):
        base, rows, _ = MAIN[k]
        part = pl.ds(base, 3 * rows)

        def held(m8):
            return main_hbm.at[2 * m8, :, part]

        mine = own.at[:, part]
        source, at, target = {
            "x": (mine, 2 * 1, (0, 1, 0)),
            "own_up": (mine, 2 * 6, (1, 0, 0)),
            "own_down": (mine, 2 * 2, (3, 0, 0)),
            "x_up": (held(1), 2 * 7, (1, 0, 0)),
            "x_down": (held(1), 2 * 3, (3, 0, 0)),
            "far_own": (held(6), 2 * 4, (1, 0, 0)),
            "far_x": (held(3), 2 * 5, (3, 0, 0)),
            "s0": (mine, 1, (0, 0, 1)),
            **{f"s{m8}": (held(m8), 2 * m8 + 1, (0, 0, 1)) for m8 in range(1, 8)},
        }[which]
        index = KINDS.index(which)
        return pltpu.make_async_remote_copy(
            src_ref=source, dst_ref=main_hbm.at[at, :, part],
            send_sem=main_send.at[k, index], recv_sem=main_recv.at[k, index],
            device_id=(g, wide_at(*target)), device_id_type=MESH,
        )

    ARRIVALS = (
        ("x", ("x_up", "x_down", "s1")),
        ("own_up", ("far_own", "s6")),
        ("own_down", ("s2",)),
        ("x_down", ("far_x", "s3")),
        ("x_up", ("s7",)),
        ("far_own", ("s4",)),
        ("far_x", ("s5",)),
    )
    KINDS = [name for name, _ in ARRIVALS] + [f"s{m8}" for m8 in range(8)]

    def own_copy(k):
        base, rows, _ = MAIN[k]
        part = pl.ds(base, 3 * rows)
        return pltpu.make_async_copy(own.at[:, part], main_hbm.at[0, :, part], out_sem.at[3 + k])

    def send_main(k):
        base, rows, _ = MAIN[k]
        p0, p1 = means(MAIN[k])
        own[0, pl.ds(base, 3 * rows), :] = p0
        own[1, pl.ds(base, 3 * rows), :] = p1
        for which in ("x", "own_up", "own_down", "s0"):
            main_copy(k, which).start()
        own_copy(k).start()

    def pass_on(k, *arrivals):
        for name, then in ARRIVALS:
            if name in arrivals:
                main_copy(k, name).wait_recv()
                for which in then:
                    main_copy(k, which).start()

    def edge_copy(off):
        dy, fx, fc = off
        index = slot_of(*off)
        return pltpu.make_async_remote_copy(
            src_ref=slots.at[index], dst_ref=edge_hbm.at[slot_of(-dy, fx, fc)],
            send_sem=edge_send.at[index], recv_sem=edge_recv.at[slot_of(-dy, fx, fc)],
            device_id=(g, wide_at(*off)), device_id_type=MESH,
        )

    def label_copy(off):
        dy, fx, fc = off
        return pltpu.make_async_remote_copy(
            src_ref=lab, dst_ref=labels_hbm.at[slot_of(-dy, fx, fc)],
            send_sem=lab_send.at[slot_of(*off)], recv_sem=lab_recv.at[slot_of(-dy, fx, fc)],
            device_id=(g, wide_at(*off)), device_id_type=MESH,
        )

    halos = []
    for side, (other, src, dst, row_x, from_sp, to_sp) in enumerate(
        ((up, NX - M, 0, NX - 1, M + NX - 3, 1), (down, 0, M + NX, 0, M, M + NX))
    ):
        pairs = (
            (stress_hbm.at[pl.ds(0, 1), row_x], sx.at[side, pl.ds(0, 1)]),
            (stress_hbm.at[pl.ds(3, 2), row_x], sx.at[side, pl.ds(1, 2)]),
            (visc_hbm.at[pl.ds(src, M)], vi.at[pl.ds(dst, M)]),
            (vel_hbm.at[:, pl.ds(src, M)], u0.at[:, pl.ds(dst, M)]),
            (sp.at[:, pl.ds(from_sp, 3)], sp.at[:, pl.ds(to_sp, 3)]),
        )
        for i, (s, t) in enumerate(pairs):
            halos.append(
                pltpu.make_async_remote_copy(
                    src_ref=s, dst_ref=t,
                    send_sem=halo_send.at[side, i], recv_sem=halo_recv.at[side, i],
                    device_id=(other, wd), device_id_type=MESH,
                )
            )

    for copy in loads:
        copy.wait()
    force(M, 4)
    force(M + NX - 4, 4)
    lane = lax.broadcasted_iota(jnp.int32, (1, 128), 1)
    lab[...] = jnp.where(lane == 0, owner_ref[0, 0], owner_ref[0, 1])
    mask0 = mask_ref[0, 0].astype(F32)
    mask1 = mask_ref[0, 1].astype(F32)
    target0 = owner_ref[0, 0] // CP_DEV
    target1 = owner_ref[0, 1] // CP_DEV

    pl.semaphore_wait(barrier, len(others) + 2)
    for copy in halos:
        copy.start()

    faces(5, 18)
    force(8, 15)
    sweep(u0, u1, 5, 18)
    sweep(u1, u2, 6, 16)
    sweep(u2, u3, 7, 14)
    restrict(8, 12)
    send_main(0)
    for off in others:
        label_copy(off).start()
    own_label = pltpu.make_async_copy(lab, labels_hbm.at[0], out_sem.at[1])
    own_label.start()
    faces(23, 24)
    force(23, 24)
    sweep(u0, u1, 23, 24)
    sweep(u1, u2, 22, 24)
    sweep(u2, u3, 21, 24)
    restrict(20, 24)
    send_main(1)
    faces(47, 20)
    force(47, 17)
    sweep(u0, u1, 47, 20)
    sweep(u1, u2, 46, 20)
    sweep(u2, u3, 45, 20)
    restrict(44, 20)
    send_main(2)
    pass_on(0, "x", "own_up", "own_down")
    pass_on(1, "x", "own_up", "own_down")

    for copy in halos:
        copy.wait()
    inside_low = jnp.where(g > 0, 1.0, 0.0)
    inside_high = jnp.where(g < n_grp - 1, 1.0, 0.0)
    for at, inside in ((0, inside_low), (M + NX, inside_high)):
        here = pl.ds(at, M)
        u0[:, here] = u0[:, here] * inside
        vi[here] = vi[here] * inside
    for c, comp in enumerate(DX_COMPS):
        sp[c, M] = sp[c, M] - (0.5 * inside_low) * sx[0, c]
        sp[c, M + NX - 1] = sp[c, M + NX - 1] + (0.5 * inside_high) * sx[1, c]
        sp[c, M - 1] = sp[c, M - 1] + 0.5 * st[comp, 1]
        sp[c, M + NX] = sp[c, M + NX] - 0.5 * st[comp, NX]
    faces(1, 3, inside_low)
    faces(M + NX, 3, inside_high)
    faces(M, 1)
    faces(M + NX - 1, 1)
    for src, dst, shift in ((u0, u1, 1), (u1, u2, 2), (u2, u3, 3)):
        sweep(src, dst, shift, 4)
        sweep(src, dst, EX - 4 - shift, 4)
    store = pltpu.make_async_copy(u3.at[:, pl.ds(M, NX)], newvel_hbm, out_sem.at[0])
    store.start()
    restrict(M, 4)
    restrict(M + NX - 4, 4)
    p0, p1 = means(EDGE)
    for off in others + [(0, 0, 0)]:
        t = wide_at(*off)
        s0 = jnp.where(target0 == t, 1.0, 0.0)
        s1 = jnp.where(target1 == t, 1.0, 0.0)
        slots[slot_of(*off)] = p0 * s0 + p1 * s1
        if off != (0, 0, 0):
            edge_copy(off).start()
    own_edge = pltpu.make_async_copy(slots.at[0], edge_hbm.at[0], out_sem.at[2])
    own_edge.start()

    pass_on(2, "x", "own_up", "own_down")
    for k in range(3):
        pass_on(k, "x_down", "x_up", "far_own", "far_x")
    for k in range(3):
        for which in KINDS:
            main_copy(k, which).wait_send()
        for m8 in range(8):
            main_copy(k, f"s{m8}").wait_recv()
        own_copy(k).wait()
    for off in others:
        label_copy(off).wait()
        edge_copy(off).wait()
    own_label.wait()
    own_edge.wait()
    store.wait()


def sum_kernel(labels_ref, vel_hbm, main_hbm, edge_hbm, newvel_hbm, out_ref, main, edge, main_sem, sems):
    me = lax.axis_index("wide")
    move = pltpu.make_async_copy(vel_hbm, newvel_hbm, sems.at[0])
    fetch = pltpu.make_async_copy(edge_hbm, edge, sems.at[1])
    hits = []
    for d in range(N_WIDE):
        first, second = labels_ref[d, 0, 0], labels_ref[d, 0, 1]
        hit0 = first // CP_DEV == me
        hit1 = second // CP_DEV == me
        index = jnp.where(hit0, first, second) % CP_DEV
        copy = pltpu.make_async_copy(
            main_hbm.at[d, jnp.where(hit0, 0, 1)], main.at[d], main_sem.at[d]
        )
        hits.append((hit0 | hit1, (index // 8) * 384 + index % 8, copy))

        @pl.when(hit0 | hit1)
        def _():
            copy.start()

    fetch.start()
    move.start()
    out_ref[...] = jnp.zeros_like(out_ref)
    fetch.wait()
    for d, (hit, start, copy) in enumerate(hits):

        @pl.when(hit)
        def _():
            copy.wait()
            for buffer, chunks in ((main, MAIN), (edge, (EDGE,))):
                for base, rows, pieces in chunks:
                    for c in range(3):
                        for at, tile, count in pieces:
                            where = pl.ds(start + c * 768 + tile * 8, count, stride=8)
                            out_ref[where, :] = (
                                out_ref[where, :] + buffer[d, pl.ds(base + c * rows + at, count), :]
                            )

    move.wait()


def on_device(velocity, coarse_ghost, viscosity, stress, patch_mask, coarse_owner):
    n_grp = lax.axis_size("grp")
    hbm = pl.BlockSpec(memory_space=pltpu.HBM)
    scalar_field = pltpu.VMEM((EX, 8, 128), F32)
    field = pltpu.VMEM((3, EX, 8, 128), F32)
    dma = pltpu.SemaphoreType.DMA
    operands = [
        pltpu.with_memory_space_constraint(a, pltpu.HBM)
        for a in (patch_mask, coarse_owner, velocity, coarse_ghost, viscosity, stress)
    ]
    new_velocity, main, edge, labels = pl.pallas_call(
        functools.partial(step_kernel, n_grp),
        out_shape=(
            jax.ShapeDtypeStruct((3, NX, 8, 128), F32),
            jax.ShapeDtypeStruct((N_WIDE, 2, 120, 128), F32),
            jax.ShapeDtypeStruct((N_WIDE, 24, 128), F32),
            jax.ShapeDtypeStruct((N_WIDE, 1, 128), jnp.int32),
        ),
        in_specs=[hbm] * 6,
        out_specs=(hbm,) * 4,
        scratch_shapes=[
            field, pltpu.VMEM((6, NX + 2, 8, 128), F32), pltpu.VMEM((2, 3, 8, 128), F32),
            scalar_field, pltpu.VMEM((3, NX, 2, 128), F32),
            *[scalar_field] * 9,
            field, field, field, field, field,
            pltpu.VMEM((3, 256, 128), F32), pltpu.VMEM((3, 256, 128), F32),
            pltpu.VMEM((48, 512), F32), pltpu.VMEM((512, 256), jnp.bfloat16),
            pltpu.VMEM((2, 120, 128), F32), pltpu.VMEM((N_WIDE, 24, 128), F32),
            pltpu.VMEM((1, 128), jnp.int32),
            pltpu.SMEM((1, 2), jnp.int32), pltpu.SMEM((1, 2), jnp.int32),
            dma((6,)),
            dma((2, 5)), dma((2, 5)),
            dma((N_WIDE,)), dma((N_WIDE,)), dma((N_WIDE,)), dma((N_WIDE,)),
            dma((3, 15)), dma((3, 15)),
            dma((6,)),
        ],
        compiler_params=pltpu.CompilerParams(
            collective_id=0, has_side_effects=True, vmem_limit_bytes=40 << 20
        ),
        name="smooth_and_send",
    )(*operands)
    new_velocity, coarse = pl.pallas_call(
        sum_kernel,
        out_shape=(
            jax.ShapeDtypeStruct((3, NX, 8, 128), F32),
            jax.ShapeDtypeStruct((2304, 128), F32),
        ),
        in_specs=[pl.BlockSpec(memory_space=pltpu.SMEM), hbm, hbm, hbm],
        out_specs=(hbm, pl.BlockSpec(memory_space=pltpu.VMEM)),
        scratch_shapes=[
            pltpu.VMEM((N_WIDE, 120, 128), F32), pltpu.VMEM((N_WIDE, 24, 128), F32),
            dma((N_WIDE,)), dma((2,)),
        ],
        compiler_params=pltpu.CompilerParams(vmem_limit_bytes=40 << 20),
        name="sum_on_owners",
    )(labels, new_velocity, main, edge)
    coarse = coarse.reshape(3, 2, 48, 8, 128).transpose(1, 3, 0, 2, 4)
    return new_velocity, coarse.reshape(1, CP_DEV, 3, 48 * 128)


def solution(mesh):
    in_specs = (
        P(None, "grp", "wide", None),
        P(None, "grp", "wide", None),
        P("grp", "wide", None),
        P(None, "grp", "wide", None),
        P("grp", "wide"),
        P("grp", "wide"),
    )
    out_specs = (P(None, "grp", "wide", None), P("grp", "wide", None, None))
    return jax.shard_map(
        on_device, mesh=mesh, in_specs=in_specs, out_specs=out_specs, check_vma=False
    )
```

time: 46 us -> 36.4 us (0.79)
  local copies, waits for them, and re-layouts: 5.72 us -> 0 us
  Pallas kernels: 39.4 us -> 35.7 us
    unnamed x12 -> x0, local copies, waits for them, and re-layouts: 5.72 us -> none
    pallas_call x2, Pallas kernels: 39.4 us -> 35.7 us  [the longest x1 32.2 us: on_device(): pl.pallas_call(functools.partial(step_kernel, n_grp), out_shape=(jax.Shap...]
where the time goes in v2:
time: 36.4 us; the launch traced here: 36.3 us
  Pallas kernels  35.7 us (98%)
  between operations  0.64 us (2%)
    pallas_call x1, Pallas kernels, on_device(): pl.pallas_call(functools.partial(step_kernel, n_grp), out_shape=(jax.Shap...  32.2 us
    pallas_call x1, Pallas kernels, on_device(): pl.pallas_call(sum_kernel, out_shape=(jax.ShapeDtypeStruct((3, NX, 8, 128...  3.47 us

profile of v2, /device:TPU:1, one launch (start us, length us, event | category | flops | bytes accessed | tf_op | source)
XLA Modules:
  0.0 36.3 jit_solution(11745355708552730689)
XLA Ops:
  0.6 32.2 %smooth_and_send.1 = (f32[3,64,8,128]{3,2,1,0:T(8,128)S(1)}, f32[16,2,120,128]{3,2,1,0:T(8,128)S(1)}, f32[16,24,128]{2,1,0:T(8,128)S(1)}, s32[16,1,128]{2,1,0:T(1,128)S(1)}) custom-call(s32[1,2]{1,0:T(1,128)} %mask_hbm.1, s32[1,2]{1,0:T(1,128)} %owner_hbm.1, f32[3,64,8,128]{3,2,1,0:T(8,128)} %vel_hbm.1, f32[3,64,2,128]{3,2,1,0:T(2,128)} %ghost_hbm.1, ...), custom_call_target="tpu_custom_call" | custom-call | tf_op jit(solution)/shard_map/smooth_and_send/pallas_call | solution.py:437
  32.8 3.5 %sum_on_owners.1 = (f32[3,64,8,128]{3,2,1,0:T(8,128)}, f32[2304,128]{1,0:T(8,128)}) custom-call(s32[16,1,128]{2,1,0:T(1,128)S(1)} %get-tuple-element.8.labels_ref, f32[3,64,8,128]{3,2,1,0:T(8,128)S(1)} %get-tuple-element.9.vel_hbm, f32[16,2,120,128]{3,2,1,0:T(8,128)S(1)} %get-tuple-element.10.main_hbm, f32[16,24,128]{2,1,0:T(8,128)S(1)} %get-tuple-element.11.edge_hbm), custom_call_target="tpu_custom_call" | custom-call | tf_op jit(solution)/shard_map/sum_on_owners/pallas_call | solution.py:468

commit v3 on v2

--- a/solution.py
+++ b/solution.py
@@ -270,15 +270,20 @@
         )
 
     halos = []
-    for side, (other, src, dst, row_x, from_sp, to_sp) in enumerate(
-        ((up, NX - M, 0, NX - 1, M + NX - 3, 1), (down, 0, M + NX, 0, M, M + NX))
+    for side, (other, row_x, visc_at, vel_at, from_sp, from_u1, to) in enumerate(
+        (
+            (up, NX - 1, NX - 3, NX - 2, M + NX - 2, M + NX - 3, (1, 2, 2, 1)),
+            (down, 0, 0, 0, M, M + 1, (M + NX, M + NX, M + NX, M + NX + 1)),
+        )
     ):
+        to_visc, to_vel, to_sp, to_u1 = to
         pairs = (
+            (u1.at[:, pl.ds(from_u1, 2)], u1.at[:, pl.ds(to_u1, 2)]),
             (stress_hbm.at[pl.ds(0, 1), row_x], sx.at[side, pl.ds(0, 1)]),
             (stress_hbm.at[pl.ds(3, 2), row_x], sx.at[side, pl.ds(1, 2)]),
-            (visc_hbm.at[pl.ds(src, M)], vi.at[pl.ds(dst, M)]),
-            (vel_hbm.at[:, pl.ds(src, M)], u0.at[:, pl.ds(dst, M)]),
-            (sp.at[:, pl.ds(from_sp, 3)], sp.at[:, pl.ds(to_sp, 3)]),
+            (visc_hbm.at[pl.ds(visc_at, 3)], vi.at[pl.ds(to_visc, 3)]),
+            (vel_hbm.at[:, pl.ds(vel_at, 2)], u0.at[:, pl.ds(to_vel, 2)]),
+            (sp.at[:, pl.ds(from_sp, 2)], sp.at[:, pl.ds(to_sp, 2)]),
         )
         for i, (s, t) in enumerate(pairs):
             halos.append(
@@ -301,18 +306,23 @@
     target1 = owner_ref[0, 1] // CP_DEV
 
     pl.semaphore_wait(barrier, len(others) + 2)
-    for copy in halos:
-        copy.start()
-
-    faces(5, 18)
+    for i, copy in enumerate(halos):
+        if i % 6:
+            copy.start()
+    faces(5, 2)
+    faces(M + NX - 3, 2)
+    sweep(u0, u1, 5, 2)
+    sweep(u0, u1, M + NX - 3, 2)
+    halos[0].start()
+    halos[6].start()
+
+    faces(7, 16)
     force(8, 15)
-    sweep(u0, u1, 5, 18)
+    sweep(u0, u1, 7, 16)
     sweep(u1, u2, 6, 16)
     sweep(u2, u3, 7, 14)
     restrict(8, 12)
     send_main(0)
-    for off in others:
-        label_copy(off).start()
     own_label = pltpu.make_async_copy(lab, labels_hbm.at[0], out_sem.at[1])
     own_label.start()
     faces(23, 24)
@@ -322,9 +332,9 @@
     sweep(u2, u3, 21, 24)
     restrict(20, 24)
     send_main(1)
-    faces(47, 20)
+    faces(47, 18)
     force(47, 17)
-    sweep(u0, u1, 47, 20)
+    sweep(u0, u1, 47, 18)
     sweep(u1, u2, 46, 20)
     sweep(u2, u3, 45, 20)
     restrict(44, 20)
@@ -336,20 +346,25 @@
         copy.wait()
     inside_low = jnp.where(g > 0, 1.0, 0.0)
     inside_high = jnp.where(g < n_grp - 1, 1.0, 0.0)
-    for at, inside in ((0, inside_low), (M + NX, inside_high)):
-        here = pl.ds(at, M)
+    for at, swept, inside in ((1, 1, inside_low), (M + NX, M + NX + 1, inside_high)):
+        here = pl.ds(swept, 2)
+        u1[:, here] = u1[:, here] * inside
+        here = pl.ds(2 if at == 1 else at, 2)
         u0[:, here] = u0[:, here] * inside
+        here = pl.ds(at, 3)
         vi[here] = vi[here] * inside
     for c, comp in enumerate(DX_COMPS):
         sp[c, M] = sp[c, M] - (0.5 * inside_low) * sx[0, c]
         sp[c, M + NX - 1] = sp[c, M + NX - 1] + (0.5 * inside_high) * sx[1, c]
         sp[c, M - 1] = sp[c, M - 1] + 0.5 * st[comp, 1]
         sp[c, M + NX] = sp[c, M + NX] - 0.5 * st[comp, NX]
-    faces(1, 3, inside_low)
-    faces(M + NX, 3, inside_high)
+    faces(2, 2, inside_low)
+    faces(M + NX, 2, inside_high)
     faces(M, 1)
     faces(M + NX - 1, 1)
-    for src, dst, shift in ((u0, u1, 1), (u1, u2, 2), (u2, u3, 3)):
+    sweep(u0, u1, 3, 2)
+    sweep(u0, u1, M + NX - 1, 2)
+    for src, dst, shift in ((u1, u2, 2), (u2, u3, 3)):
         sweep(src, dst, shift, 4)
         sweep(src, dst, EX - 4 - shift, 4)
     store = pltpu.make_async_copy(u3.at[:, pl.ds(M, NX)], newvel_hbm, out_sem.at[0])
@@ -366,10 +381,14 @@
             edge_copy(off).start()
     own_edge = pltpu.make_async_copy(slots.at[0], edge_hbm.at[0], out_sem.at[2])
     own_edge.start()
+    for off in others:
+        label_copy(off).start()
 
     pass_on(2, "x", "own_up", "own_down")
     for k in range(3):
-        pass_on(k, "x_down", "x_up", "far_own", "far_x")
+        pass_on(k, "x_down", "x_up")
+    for k in range(3):
+        pass_on(k, "far_own", "far_x")
     for k in range(3):
         for which in KINDS:
             main_copy(k, which).wait_send()
@@ -384,49 +403,45 @@
     store.wait()
 
 
-def sum_kernel(labels_ref, vel_hbm, main_hbm, edge_hbm, newvel_hbm, out_ref, main, edge, main_sem, sems):
+def sum_kernel(labels_ref, vel_hbm, main, edge, newvel_hbm, out_hbm, total, laid_out, sems):
     me = lax.axis_index("wide")
-    move = pltpu.make_async_copy(vel_hbm, newvel_hbm, sems.at[0])
-    fetch = pltpu.make_async_copy(edge_hbm, edge, sems.at[1])
-    hits = []
+    move = pltpu.make_async_copy(vel_hbm, newvel_hbm, sems.at[3])
+    move.start()
+    total[...] = jnp.zeros_like(total)
     for d in range(N_WIDE):
         first, second = labels_ref[d, 0, 0], labels_ref[d, 0, 1]
         hit0 = first // CP_DEV == me
         hit1 = second // CP_DEV == me
         index = jnp.where(hit0, first, second) % CP_DEV
-        copy = pltpu.make_async_copy(
-            main_hbm.at[d, jnp.where(hit0, 0, 1)], main.at[d], main_sem.at[d]
-        )
-        hits.append((hit0 | hit1, (index // 8) * 384 + index % 8, copy))
+        patch = jnp.where(hit0, 0, 1)
 
         @pl.when(hit0 | hit1)
         def _():
-            copy.start()
-
-    fetch.start()
-    move.start()
-    out_ref[...] = jnp.zeros_like(out_ref)
-    fetch.wait()
-    for d, (hit, start, copy) in enumerate(hits):
-
-        @pl.when(hit)
-        def _():
-            copy.wait()
-            for buffer, chunks in ((main, MAIN), (edge, (EDGE,))):
+            total[index, :120] = total[index, :120] + main[d, patch]
+            total[index, 120:] = total[index, 120:] + edge[d]
+
+    stores = []
+    for c in range(3):
+        for k in range(CP_DEV):
+            start = c * 768 + (k // 8) * 384 + k % 8
+            for first_row, chunks in ((0, MAIN), (120, (EDGE,))):
                 for base, rows, pieces in chunks:
-                    for c in range(3):
-                        for at, tile, count in pieces:
-                            where = pl.ds(start + c * 768 + tile * 8, count, stride=8)
-                            out_ref[where, :] = (
-                                out_ref[where, :] + buffer[d, pl.ds(base + c * rows + at, count), :]
-                            )
-
+                    for at, tile, count in pieces:
+                        laid_out[pl.ds(start + tile * 8, count, stride=8), :] = total[
+                            k, pl.ds(first_row + base + c * rows + at, count), :
+                        ]
+        part = pl.ds(c * 768, 768)
+        stores.append(pltpu.make_async_copy(laid_out.at[part], out_hbm.at[part], sems.at[c]))
+        stores[-1].start()
+    for store in stores:
+        store.wait()
     move.wait()
 
 
 def on_device(velocity, coarse_ghost, viscosity, stress, patch_mask, coarse_owner):
     n_grp = lax.axis_size("grp")
     hbm = pl.BlockSpec(memory_space=pltpu.HBM)
+    vmem = pl.BlockSpec(memory_space=pltpu.VMEM)
     scalar_field = pltpu.VMEM((EX, 8, 128), F32)
     field = pltpu.VMEM((3, EX, 8, 128), F32)
     dma = pltpu.SemaphoreType.DMA
@@ -455,7 +470,7 @@
             pltpu.VMEM((1, 128), jnp.int32),
             pltpu.SMEM((1, 2), jnp.int32), pltpu.SMEM((1, 2), jnp.int32),
             dma((6,)),
-            dma((2, 5)), dma((2, 5)),
+            dma((2, 6)), dma((2, 6)),
             dma((N_WIDE,)), dma((N_WIDE,)), dma((N_WIDE,)), dma((N_WIDE,)),
             dma((3, 15)), dma((3, 15)),
             dma((6,)),
@@ -471,11 +486,10 @@
             jax.ShapeDtypeStruct((3, NX, 8, 128), F32),
             jax.ShapeDtypeStruct((2304, 128), F32),
         ),
-        in_specs=[pl.BlockSpec(memory_space=pltpu.SMEM), hbm, hbm, hbm],
-        out_specs=(hbm, pl.BlockSpec(memory_space=pltpu.VMEM)),
+        in_specs=[pl.BlockSpec(memory_space=pltpu.SMEM), hbm, vmem, vmem],
+        out_specs=(hbm, hbm),
         scratch_shapes=[
-            pltpu.VMEM((N_WIDE, 120, 128), F32), pltpu.VMEM((N_WIDE, 24, 128), F32),
-            dma((N_WIDE,)), dma((2,)),
+            pltpu.VMEM((CP_DEV, 144, 128), F32), pltpu.VMEM((2304, 128), F32), dma((4,)),
         ],
         compiler_params=pltpu.CompilerParams(vmem_limit_bytes=40 << 20),
         name="sum_on_owners",

time: 36.4 us -> 32.2 us (0.88)
  Pallas kernels: 35.7 us -> 31.4 us
    pallas_call x1, Pallas kernels: 32.2 us -> 29.1 us  [on_device(): pl.pallas_call(functools.partial(step_kernel, n_grp), out_shape=(jax.Shap...]
    pallas_call x1, Pallas kernels: 3.47 us -> 2.29 us  [on_device(): pl.pallas_call(sum_kernel, out_shape=(jax.ShapeDtypeStruct((3, NX, 8, 128...]
where the time goes in v3:
time: 32.2 us; the launch traced here: 32.1 us
  Pallas kernels  31.4 us (98%)
  between operations  0.64 us (2%)
    pallas_call x1, Pallas kernels, on_device(): pl.pallas_call(functools.partial(step_kernel, n_grp), out_shape=(jax.Shap...  29.1 us
    pallas_call x1, Pallas kernels, on_device(): pl.pallas_call(sum_kernel, out_shape=(jax.ShapeDtypeStruct((3, NX, 8, 128...  2.29 us

profile of v3, /device:TPU:1, one launch (start us, length us, event | category | flops | bytes accessed | tf_op | source)
XLA Modules:
  0.0 32.1 jit_solution(13032181932475427799)
XLA Ops:
  0.6 29.1 %smooth_and_send.1 = (f32[3,64,8,128]{3,2,1,0:T(8,128)S(1)}, f32[16,2,120,128]{3,2,1,0:T(8,128)S(1)}, f32[16,24,128]{2,1,0:T(8,128)S(1)}, s32[16,1,128]{2,1,0:T(1,128)S(1)}) custom-call(s32[1,2]{1,0:T(1,128)} %mask_hbm.1, s32[1,2]{1,0:T(1,128)} %owner_hbm.1, f32[3,64,8,128]{3,2,1,0:T(8,128)} %vel_hbm.1, f32[3,64,2,128]{3,2,1,0:T(2,128)} %ghost_hbm.1, ...), custom_call_target="tpu_custom_call" | custom-call | tf_op jit(solution)/shard_map/smooth_and_send/pallas_call | solution.py:452
  29.8 2.3 %sum_on_owners.1 = (f32[3,64,8,128]{3,2,1,0:T(8,128)}, f32[2304,128]{1,0:T(8,128)}) custom-call(s32[16,1,128]{2,1,0:T(1,128)S(1)} %get-tuple-element.8.labels_ref, f32[3,64,8,128]{3,2,1,0:T(8,128)S(1)} %get-tuple-element.9.vel_hbm, f32[16,2,120,128]{3,2,1,0:T(8,128)S(1)} %get-tuple-element.10.main, f32[16,24,128]{2,1,0:T(8,128)S(1)} %get-tuple-element.11.edge), custom_call_target="tpu_custom_call" | custom-call | tf_op jit(solution)/shard_map/sum_on_owners/pallas_call | solution.py:483

commit v4 on v3

--- a/solution.py
+++ b/solution.py
@@ -20,9 +20,9 @@
 DX_COMPS = (0, 3, 4)
 
 MAIN = (
-    (0, 8, ((0, 2, 6), (6, 33, 1), (7, 41, 1))),
-    (24, 16, ((0, 8, 8), (8, 16, 4), (12, 34, 2), (14, 42, 2))),
-    (72, 16, ((0, 20, 8), (8, 28, 2), (10, 36, 3), (13, 44, 3))),
+    (0, 16, ((0, 2, 8), (8, 10, 4), (12, 33, 2), (14, 41, 2))),
+    (48, 16, ((0, 14, 8), (8, 22, 2), (10, 35, 3), (13, 43, 3))),
+    (96, 8, ((0, 24, 6), (6, 38, 1), (7, 46, 1))),
 )
 EDGE = (0, 8, ((0, 0, 2), (2, 30, 2), (4, 32, 1), (5, 39, 1), (6, 40, 1), (7, 47, 1)))
 
@@ -316,31 +316,32 @@
     halos[0].start()
     halos[6].start()
 
-    faces(7, 16)
-    force(8, 15)
-    sweep(u0, u1, 7, 16)
-    sweep(u1, u2, 6, 16)
-    sweep(u2, u3, 7, 14)
-    restrict(8, 12)
+    faces(7, 28)
+    force(8, 27)
+    sweep(u0, u1, 7, 28)
+    sweep(u1, u2, 6, 28)
+    sweep(u2, u3, 7, 26)
+    restrict(8, 24)
     send_main(0)
     own_label = pltpu.make_async_copy(lab, labels_hbm.at[0], out_sem.at[1])
     own_label.start()
-    faces(23, 24)
-    force(23, 24)
-    sweep(u0, u1, 23, 24)
-    sweep(u1, u2, 22, 24)
-    sweep(u2, u3, 21, 24)
-    restrict(20, 24)
+    faces(35, 20)
+    force(35, 20)
+    sweep(u0, u1, 35, 20)
+    sweep(u1, u2, 34, 20)
+    sweep(u2, u3, 33, 20)
+    restrict(32, 20)
     send_main(1)
-    faces(47, 18)
-    force(47, 17)
-    sweep(u0, u1, 47, 18)
-    sweep(u1, u2, 46, 20)
-    sweep(u2, u3, 45, 20)
-    restrict(44, 20)
+    faces(55, 10)
+    force(55, 9)
+    sweep(u0, u1, 55, 10)
+    sweep(u1, u2, 54, 12)
+    sweep(u2, u3, 53, 12)
+    restrict(52, 12)
     send_main(2)
     pass_on(0, "x", "own_up", "own_down")
     pass_on(1, "x", "own_up", "own_down")
+    pass_on(2, "x", "own_up", "own_down")
 
     for copy in halos:
         copy.wait()
@@ -384,7 +385,6 @@
     for off in others:
         label_copy(off).start()
 
-    pass_on(2, "x", "own_up", "own_down")
     for k in range(3):
         pass_on(k, "x_down", "x_up")
     for k in range(3):

time: 32.2 us -> 31.1 us (0.966)
  Pallas kernels: 31.4 us -> 30.3 us
    pallas_call x1, Pallas kernels: 29.1 us -> 28.1 us  [on_device(): pl.pallas_call(functools.partial(step_kernel, n_grp), out_shape=(jax.Shap...]
where the time goes in v4:
time: 31.1 us; the launch traced here: 31 us
  Pallas kernels  30.3 us (97%)
  between operations  0.64 us (2%)
    pallas_call x1, Pallas kernels, on_device(): pl.pallas_call(functools.partial(step_kernel, n_grp), out_shape=(jax.Shap...  28.1 us
    pallas_call x1, Pallas kernels, on_device(): pl.pallas_call(sum_kernel, out_shape=(jax.ShapeDtypeStruct((3, NX, 8, 128...  2.29 us

profile of v4, /device:TPU:1, one launch (start us, length us, event | category | flops | bytes accessed | tf_op | source)
XLA Modules:
  0.0 31.0 jit_solution(18174581034998902128)
XLA Ops:
  0.6 28.1 %smooth_and_send.1 = (f32[3,64,8,128]{3,2,1,0:T(8,128)S(1)}, f32[16,2,120,128]{3,2,1,0:T(8,128)S(1)}, f32[16,24,128]{2,1,0:T(8,128)S(1)}, s32[16,1,128]{2,1,0:T(1,128)S(1)}) custom-call(s32[1,2]{1,0:T(1,128)} %mask_hbm.1, s32[1,2]{1,0:T(1,128)} %owner_hbm.1, f32[3,64,8,128]{3,2,1,0:T(8,128)} %vel_hbm.1, f32[3,64,2,128]{3,2,1,0:T(2,128)} %ghost_hbm.1, ...), custom_call_target="tpu_custom_call" | custom-call | tf_op jit(solution)/shard_map/smooth_and_send/pallas_call | solution.py:452
  28.7 2.3 %sum_on_owners.1 = (f32[3,64,8,128]{3,2,1,0:T(8,128)}, f32[2304,128]{1,0:T(8,128)}) custom-call(s32[16,1,128]{2,1,0:T(1,128)S(1)} %get-tuple-element.8.labels_ref, f32[3,64,8,128]{3,2,1,0:T(8,128)S(1)} %get-tuple-element.9.vel_hbm, f32[16,2,120,128]{3,2,1,0:T(8,128)S(1)} %get-tuple-element.10.main, f32[16,24,128]{2,1,0:T(8,128)S(1)} %get-tuple-element.11.edge), custom_call_target="tpu_custom_call" | custom-call | tf_op jit(solution)/shard_map/sum_on_owners/pallas_call | solution.py:483

commit v5 on v3

--- a/solution.py
+++ b/solution.py
@@ -20,8 +20,7 @@
 DX_COMPS = (0, 3, 4)
 
 MAIN = (
-    (0, 8, ((0, 2, 6), (6, 33, 1), (7, 41, 1))),
-    (24, 16, ((0, 8, 8), (8, 16, 4), (12, 34, 2), (14, 42, 2))),
+    (0, 24, ((0, 2, 8), (8, 10, 8), (16, 18, 2), (18, 33, 3), (21, 41, 3))),
     (72, 16, ((0, 20, 8), (8, 28, 2), (10, 36, 3), (13, 44, 3))),
 )
 EDGE = (0, 8, ((0, 0, 2), (2, 30, 2), (4, 32, 1), (5, 39, 1), (6, 40, 1), (7, 47, 1)))
@@ -316,29 +315,22 @@
     halos[0].start()
     halos[6].start()
 
-    faces(7, 16)
-    force(8, 15)
-    sweep(u0, u1, 7, 16)
-    sweep(u1, u2, 6, 16)
-    sweep(u2, u3, 7, 14)
-    restrict(8, 12)
+    faces(7, 40)
+    force(8, 39)
+    sweep(u0, u1, 7, 40)
+    sweep(u1, u2, 6, 40)
+    sweep(u2, u3, 7, 38)
+    restrict(8, 36)
     send_main(0)
     own_label = pltpu.make_async_copy(lab, labels_hbm.at[0], out_sem.at[1])
     own_label.start()
-    faces(23, 24)
-    force(23, 24)
-    sweep(u0, u1, 23, 24)
-    sweep(u1, u2, 22, 24)
-    sweep(u2, u3, 21, 24)
-    restrict(20, 24)
-    send_main(1)
     faces(47, 18)
     force(47, 17)
     sweep(u0, u1, 47, 18)
     sweep(u1, u2, 46, 20)
     sweep(u2, u3, 45, 20)
     restrict(44, 20)
-    send_main(2)
+    send_main(1)
     pass_on(0, "x", "own_up", "own_down")
     pass_on(1, "x", "own_up", "own_down")
 
@@ -384,12 +376,11 @@
     for off in others:
         label_copy(off).start()
 
-    pass_on(2, "x", "own_up", "own_down")
-    for k in range(3):
+    for k in range(len(MAIN)):
         pass_on(k, "x_down", "x_up")
-    for k in range(3):
+    for k in range(len(MAIN)):
         pass_on(k, "far_own", "far_x")
-    for k in range(3):
+    for k in range(len(MAIN)):
         for which in KINDS:
             main_copy(k, which).wait_send()
         for m8 in range(8):
@@ -465,14 +456,14 @@
             *[scalar_field] * 9,
             field, field, field, field, field,
             pltpu.VMEM((3, 256, 128), F32), pltpu.VMEM((3, 256, 128), F32),
-            pltpu.VMEM((48, 512), F32), pltpu.VMEM((512, 256), jnp.bfloat16),
+            pltpu.VMEM((96, 512), F32), pltpu.VMEM((512, 256), jnp.bfloat16),
             pltpu.VMEM((2, 120, 128), F32), pltpu.VMEM((N_WIDE, 24, 128), F32),
             pltpu.VMEM((1, 128), jnp.int32),
             pltpu.SMEM((1, 2), jnp.int32), pltpu.SMEM((1, 2), jnp.int32),
             dma((6,)),
             dma((2, 6)), dma((2, 6)),
             dma((N_WIDE,)), dma((N_WIDE,)), dma((N_WIDE,)), dma((N_WIDE,)),
-            dma((3, 15)), dma((3, 15)),
+            dma((2, 15)), dma((2, 15)),
             dma((6,)),
         ],
         compiler_params=pltpu.CompilerParams(

time: 32.2 us -> 30.7 us (0.953)
  Pallas kernels: 31.4 us -> 30 us
    pallas_call x1, Pallas kernels: 29.1 us -> 27.7 us  [on_device(): pl.pallas_call(functools.partial(step_kernel, n_grp), out_shape=(jax.Shap...]
where the time goes in v5:
time: 30.7 us; the launch traced here: 30.6 us
  Pallas kernels  30 us (98%)
  between operations  0.64 us (2%)
    pallas_call x1, Pallas kernels, on_device(): pl.pallas_call(functools.partial(step_kernel, n_grp), out_shape=(jax.Shap...  27.7 us
    pallas_call x1, Pallas kernels, on_device(): pl.pallas_call(sum_kernel, out_shape=(jax.ShapeDtypeStruct((3, NX, 8, 128...  2.25 us

profile of v5, /device:TPU:1, one launch (start us, length us, event | category | flops | bytes accessed | tf_op | source)
XLA Modules:
  0.0 30.6 jit_solution(13867360959264852647)
XLA Ops:
  0.6 27.7 %smooth_and_send.1 = (f32[3,64,8,128]{3,2,1,0:T(8,128)S(1)}, f32[16,2,120,128]{3,2,1,0:T(8,128)S(1)}, f32[16,24,128]{2,1,0:T(8,128)S(1)}, s32[16,1,128]{2,1,0:T(1,128)S(1)}) custom-call(s32[1,2]{1,0:T(1,128)} %mask_hbm.1, s32[1,2]{1,0:T(1,128)} %owner_hbm.1, f32[3,64,8,128]{3,2,1,0:T(8,128)} %vel_hbm.1, f32[3,64,2,128]{3,2,1,0:T(2,128)} %ghost_hbm.1, ...), custom_call_target="tpu_custom_call" | custom-call | tf_op jit(solution)/shard_map/smooth_and_send/pallas_call | solution.py:443
  28.4 2.2 %sum_on_owners.1 = (f32[3,64,8,128]{3,2,1,0:T(8,128)}, f32[2304,128]{1,0:T(8,128)}) custom-call(s32[16,1,128]{2,1,0:T(1,128)S(1)} %get-tuple-element.8.labels_ref, f32[3,64,8,128]{3,2,1,0:T(8,128)S(1)} %get-tuple-element.9.vel_hbm, f32[16,2,120,128]{3,2,1,0:T(8,128)S(1)} %get-tuple-element.10.main, f32[16,24,128]{2,1,0:T(8,128)S(1)} %get-tuple-element.11.edge), custom_call_target="tpu_custom_call" | custom-call | tf_op jit(solution)/shard_map/sum_on_owners/pallas_call | solution.py:474

commit v6 on v5

--- a/solution.py
+++ b/solution.py
@@ -396,7 +396,7 @@
 
 def sum_kernel(labels_ref, vel_hbm, main, edge, newvel_hbm, out_hbm, total, laid_out, sems):
     me = lax.axis_index("wide")
-    move = pltpu.make_async_copy(vel_hbm, newvel_hbm, sems.at[3])
+    move = pltpu.make_async_copy(vel_hbm, newvel_hbm, sems.at[6])
     move.start()
     total[...] = jnp.zeros_like(total)
     for d in range(N_WIDE):
@@ -412,17 +412,18 @@
             total[index, 120:] = total[index, 120:] + edge[d]
 
     stores = []
-    for c in range(3):
-        for k in range(CP_DEV):
-            start = c * 768 + (k // 8) * 384 + k % 8
+    for piece in range(6):
+        c, half = piece // 2, piece % 2
+        for k in range(8 * half, 8 * half + 8):
+            start = piece * 384 + k % 8
             for first_row, chunks in ((0, MAIN), (120, (EDGE,))):
                 for base, rows, pieces in chunks:
                     for at, tile, count in pieces:
                         laid_out[pl.ds(start + tile * 8, count, stride=8), :] = total[
                             k, pl.ds(first_row + base + c * rows + at, count), :
                         ]
-        part = pl.ds(c * 768, 768)
-        stores.append(pltpu.make_async_copy(laid_out.at[part], out_hbm.at[part], sems.at[c]))
+        part = pl.ds(piece * 384, 384)
+        stores.append(pltpu.make_async_copy(laid_out.at[part], out_hbm.at[part], sems.at[piece]))
         stores[-1].start()
     for store in stores:
         store.wait()
@@ -480,7 +481,7 @@
         in_specs=[pl.BlockSpec(memory_space=pltpu.SMEM), hbm, vmem, vmem],
         out_specs=(hbm, hbm),
         scratch_shapes=[
-            pltpu.VMEM((CP_DEV, 144, 128), F32), pltpu.VMEM((2304, 128), F32), dma((4,)),
+            pltpu.VMEM((CP_DEV, 144, 128), F32), pltpu.VMEM((2304, 128), F32), dma((7,)),
         ],
         compiler_params=pltpu.CompilerParams(vmem_limit_bytes=40 << 20),
         name="sum_on_owners",

time: 30.7 us -> 30.7 us (level)
  no operation moved by 1% of the time
where the time goes in v6:
time: 30.7 us; the launch traced here: 30.6 us
  Pallas kernels  29.9 us (97%)
  between operations  0.64 us (2%)
    pallas_call x1, Pallas kernels, on_device(): pl.pallas_call(functools.partial(step_kernel, n_grp), out_shape=(jax.Shap...  27.7 us
    pallas_call x1, Pallas kernels, on_device(): pl.pallas_call(sum_kernel, out_shape=(jax.ShapeDtypeStruct((3, NX, 8, 128...  2.2 us

profile of v6, /device:TPU:1, one launch (start us, length us, event | category | flops | bytes accessed | tf_op | source)
XLA Modules:
  0.0 30.6 jit_solution(10770890693632458090)
XLA Ops:
  0.6 27.7 %smooth_and_send.1 = (f32[3,64,8,128]{3,2,1,0:T(8,128)S(1)}, f32[16,2,120,128]{3,2,1,0:T(8,128)S(1)}, f32[16,24,128]{2,1,0:T(8,128)S(1)}, s32[16,1,128]{2,1,0:T(1,128)S(1)}) custom-call(s32[1,2]{1,0:T(1,128)} %mask_hbm.1, s32[1,2]{1,0:T(1,128)} %owner_hbm.1, f32[3,64,8,128]{3,2,1,0:T(8,128)} %vel_hbm.1, f32[3,64,2,128]{3,2,1,0:T(2,128)} %ghost_hbm.1, ...), custom_call_target="tpu_custom_call" | custom-call | tf_op jit(solution)/shard_map/smooth_and_send/pallas_call | solution.py:444
  28.4 2.2 %sum_on_owners.1 = (f32[3,64,8,128]{3,2,1,0:T(8,128)}, f32[2304,128]{1,0:T(8,128)}) custom-call(s32[16,1,128]{2,1,0:T(1,128)S(1)} %get-tuple-element.8.labels_ref, f32[3,64,8,128]{3,2,1,0:T(8,128)S(1)} %get-tuple-element.9.vel_hbm, f32[16,2,120,128]{3,2,1,0:T(8,128)S(1)} %get-tuple-element.10.main, f32[16,24,128]{2,1,0:T(8,128)S(1)} %get-tuple-element.11.edge), custom_call_target="tpu_custom_call" | custom-call | tf_op jit(solution)/shard_map/sum_on_owners/pallas_call | solution.py:475
